TPU v7x, 256 devices: a whole 4x4x8 slice. The times are simulated.
256 devices in a mesh: dom: 32 (over y_hi, z, core), hid: 8 (over y_lo, x).
Axes of the slice: x: 4, y: 4 (y_hi: 2, y_lo: 2; y = y_hi * 2 + y_lo), z: 8, core: 2. Of those that a mesh axis runs over, the one named last changes fastest.
Arguments:
- features: bfloat16 [512, 32768], P(None, 'dom'), may hold values from -6 to 6
- weight: bfloat16 [512, 512], P(None, 'hid'), may hold values from -0.25 to 0.25
- band_tiles: bfloat16 [3072, 32768], P(None, 'dom'), may hold values from -0.109375 to 0.109375
- tile_live: int32 [12, 128], P(None, 'dom'), may hold values 0 or 1
- send_rows: int32 [32, 32, 128], P('dom'), may hold values from 0 to 1023
- recv_rows: int32 [32, 32, 128], P('dom'), may hold values from 0 to 1023
- edge_weight: float32 [32, 32, 128], P('dom'), may hold values from 0.25 to 1
- live_slots: int32 [32, 32], P('dom'), may hold values from 96 to 128, as said below
- bias_terms: float32 [512], P('hid'), may hold values from -3 to 3
- cotangent: bfloat16 [512, 32768], P('hid', 'dom'), may hold values from -6 to 6
Outputs:
- output: bfloat16 [512, 32768], P('hid', 'dom')
- feature_grad: bfloat16 [512, 32768], P('hid', 'dom')
- weight_grad: float32 [512, 512], P(None, 'hid')
- bias_grad: float32 [512], P('hid')
Inputs may be any that keep to these rules, and one draw needn't show every extreme that they name: `live_slots`: every reader block has at least one owner block whose list has all 128 slots live.
All inputs are finite; a program needn't handle non-finite values. No bound on the sum of `tile_live` on one device may be relied on, other than what follows from the above.
Results may differ from a plain program's by a relative error of at most 0.0065.
Values may be sent and summed in bfloat16 or wider, within the bound.
A program may use at most 64 MiB of HBM per device.

v0:
```python
import jax
import jax.numpy as jnp
from jax import lax
from jax.sharding import PartitionSpec as P

TILE = 256


def passed_along(block, axis, distance):
    devices = range(lax.axis_size(axis))
    route = [((i - distance) % len(devices), i) for i in devices]
    return lax.ppermute(block, axis, route)


def silu_grad(value):
    gate = jax.nn.sigmoid(value)
    return gate * (1.0 + value * (1.0 - gate))


def on_device(
    features,
    weight,
    band_tiles,
    tile_live,
    send_rows,
    recv_rows,
    edge_weight,
    live_slots,
    bias_terms,
    cotangent,
):
    row_count = features.shape[1]
    local_width = weight.shape[1]
    mapped = lax.dot_general(
        weight, features, (((0,), (0,)), ((), ())), preferred_element_type=jnp.float32
    ).astype(jnp.bfloat16)
    tile_mask = tile_live.astype(jnp.bfloat16)
    dense = (
        band_tiles.reshape(3 * row_count // TILE, TILE, row_count // TILE, TILE)
        * tile_mask[:, None, :, None]
    ).reshape(3 * row_count, row_count)
    summed = jnp.dot(mapped, dense[row_count : 2 * row_count], preferred_element_type=jnp.float32)
    for offset in (0, 2):
        arrived = passed_along(mapped, "dom", 1 - offset)
        summed = summed + jnp.dot(
            arrived,
            dense[offset * row_count : (offset + 1) * row_count],
            preferred_element_type=jnp.float32,
        )
    slot_ids = jnp.arange(send_rows.shape[2])
    slot_weight = edge_weight[0] * (slot_ids[None, :] < live_slots[0][:, None]).astype(jnp.float32)
    outgoing = mapped[:, send_rows[0]]
    incoming = lax.all_to_all(outgoing, "dom", split_axis=1, concat_axis=1, tiled=True)
    weighted = incoming.astype(jnp.float32) * slot_weight[None]
    summed = summed.at[:, recv_rows[0].reshape(-1)].add(weighted.reshape(local_width, -1))
    act = summed + bias_terms[:, None]
    output = jax.nn.silu(act).astype(jnp.bfloat16)
    pre_grad = (cotangent.astype(jnp.float32) * silu_grad(act)).astype(jnp.bfloat16)
    contract = (((1,), (1,)), ((), ()))
    map_grad = lax.dot_general(
        pre_grad, dense[row_count : 2 * row_count], contract, preferred_element_type=jnp.float32
    )
    for offset in (0, 2):
        term = lax.dot_general(
            pre_grad,
            dense[offset * row_count : (offset + 1) * row_count],
            contract,
            preferred_element_type=jnp.float32,
        )
        map_grad = map_grad + passed_along(term, "dom", offset - 1)
    message = (pre_grad.astype(jnp.float32)[:, recv_rows[0]] * slot_weight[None]).astype(
        jnp.bfloat16
    )
    returned = lax.all_to_all(message, "dom", split_axis=1, concat_axis=1, tiled=True)
    map_grad = map_grad.at[:, send_rows[0].reshape(-1)].add(
        returned.astype(jnp.float32).reshape(local_width, -1)
    )
    grad_b = map_grad.astype(jnp.bfloat16)
    weight_part = lax.dot_general(features, grad_b, contract, preferred_element_type=jnp.float32)
    bias_part = jnp.sum(pre_grad.astype(jnp.float32), axis=1)
    weight_grad, bias_grad = lax.psum((weight_part, bias_part), "dom")
    feature_grad = lax.psum_scatter(
        jnp.dot(weight, grad_b, preferred_element_type=jnp.float32),
        "hid",
        scatter_dimension=0,
        tiled=True,
    ).astype(jnp.bfloat16)
    return (output, feature_grad, weight_grad, bias_grad)


def solution(mesh):
    return jax.shard_map(
        on_device,
        mesh=mesh,
        in_specs=(
            P(None, "dom"),
            P(None, "hid"),
            P(None, "dom"),
            P(None, "dom"),
            P("dom", None, None),
            P("dom", None, None),
            P("dom", None, None),
            P("dom", None),
            P("hid"),
            P("hid", "dom"),
        ),
        out_specs=(P("hid", "dom"), P("hid", "dom"), P(None, "hid"), P("hid")),
        check_vma=False,
    )
```

profile of v0, /device:TPU:1, one launch (start us, length us, event | category | flops | bytes accessed | tf_op | source)
XLA Modules:
  0.0 441.7 jit_solution(8998535476931524258)
XLA Ops:
  10.4 3.1 collective-permute-start
  14.6 12.1 %gather_fusion = bf16[4096,64]{1,0:T(8,128)(2,1)S(1)} fusion(bf16[64,1024]{0,1:T(8,128)(2,1)S(1)} %copy.31, s32[4096]{0:T(1024)S(1)} %fusion.6), kind=kCustom, calls=%fused_computation | custom fusion | bytes 1064960 | tf_op jit(solution)/shard_map/gather | solution.py:52
  27.9 12.5 %all-to-all-start = ((bf16[64,32,128]{2,0,1:T(8,128)(2,1)}), bf16[64,32,128]{2,0,1:T(8,128)(2,1)}, u32[]{:S(2)}, u32[]{:S(2)}) async-start(bf16[64,32,128]{2,0,1:T(8,128)(2,1)} %bitcast.5), calls=%async_computation | async-start | bytes 1048576 | tf_op jit(solution)/shard_map/all_to_all | solution.py:53
  40.4 11.2 %reshape.173 = bf16[12,256,4,256]{3,2,1,0:T(4,128)(2,1)} reshape(bf16[3072,1024]{1,0:T(8,128)(2,1)} %param.12) | data formatting | bytes 12582912 | tf_op jit(solution)/shard_map/reshape | solution.py:39
  51.7 8.2 %broadcast_multiply_fusion = bf16[12,256,4,256]{3,2,1,0:T(4,128)(2,1)} fusion(bf16[12,256,4,256]{3,2,1,0:T(4,128)(2,1)} %reshape.173, bf16[12,4]{1,0:T(8,128)(2,1)S(1)} %copy.30), kind=kLoop, calls=%fused_computation.4 | loop fusion | flops 3145728 | bytes 12583008 | tf_op jit(solution)/shard_map/mul | solution.py:39
  59.8 4.1 fusion.9
  65.7 2.0 copy.49
  68.4 1.8 copy.36
  76.6 1.9 copy.35
  78.5 23.1 %scatter_fusion = f32[64,1024]{0,1:T(8,128)S(1)} fusion(f32[64,1024]{0,1:T(8,128)S(1)} %copy.34, s32[4096]{0:T(1024)S(1)} %bitcast.79, f32[4096,64]{1,0:T(8,128)} %copy.35), kind=kCustom, calls=%fused_computation.2 | custom fusion | flops 262144 | bytes 3162112 | tf_op jit(solution)/shard_map/scatter-add | solution.py:55
  102.6 3.1 fusion.11
  109.0 14.2 %gather_fusion.1 = f32[4096,64]{1,0:T(8,128)} fusion(f32[64,1024]{0,1:T(8,128)S(1)} %convert_element_type.39, s32[4096]{0:T(1024)S(1)} %copy-done.9), kind=kCustom, calls=%fused_computation.1 | custom fusion | bytes 2113536 | tf_op jit(solution)/shard_map/gather | solution.py:71
  123.1 3.1 copy.37
  126.3 2.3 fusion.2
  128.6 10.5 %all-to-all-start.1 = ((bf16[64,32,128]{2,0,1:T(8,128)(2,1)}), bf16[64,32,128]{2,0,1:T(8,128)(2,1)}, u32[]{:S(2)}, u32[]{:S(2)}) async-start(bf16[64,32,128]{2,0,1:T(8,128)(2,1)} %fusion.2), calls=%async_computation.1 | async-start | bytes 1048576 | tf_op jit(solution)/shard_map/all_to_all | solution.py:74
  139.3 2.5 fusion
  142.9 14.4 %all-to-all-done.1 = bf16[64,32,128]{2,0,1:T(8,128)(2,1)} async-done(((bf16[64,32,128]{2,0,1:T(8,128)(2,1)}), bf16[64,32,128]{2,0,1:T(8,128)(2,1)}, u32[]{:S(2)}, u32[]{:S(2)}) %all-to-all-start.1) | async-done | bytes 524320 | tf_op jit(solution)/shard_map/all_to_all | solution.py:74
  158.4 1.9 copy.40
  160.4 22.9 %scatter_fusion.1 = f32[64,1024]{0,1:T(8,128)S(1)} fusion(f32[64,1024]{0,1:T(8,128)S(1)} %copy.39, s32[4096]{0:T(1024)S(1)} %bitcast.80, f32[4096,64]{1,0:T(8,128)} %copy.40), kind=kCustom, calls=%fused_computation.3 | custom fusion | flops 262144 | bytes 3162112 | tf_op jit(solution)/shard_map/scatter-add | solution.py:75
  183.3 1.7 convolution_bitcast_fusion
  185.0 2.9 copy.43
  189.9 67.3 %psum.15 = f32[64]{0:T(128)} all-reduce(f32[64]{0:T(128)S(1)} %get-tuple-element.16), channel_id=1, replica_groups=mesh['dom'=32,'hid'=8] {'dom'}, use_global_device_ids=true, to_apply=%region_5.6 | all-reduce | flops 64 | bytes 512 | tf_op jit(solution)/shard_map/psum | solution.py:81
  259.1 173.6 %all-reduce.2.cloned.1.call-done = f32[512,64]{0,1:T(8,128)} async-done(((f32[512,64]{0,1:T(8,128)}), f32[512,64]{0,1:T(8,128)}) %all-reduce.2.cloned.1.call-update) | async-done | bytes 131088 | tf_op jit(solution)/shard_map/psum | solution.py:81
  432.7 1.6 copy.55
  (67 shorter events, 24.1 us)
Async XLA Ops:
  8.0 1.2 copy-start
  10.4 62.0 %collective-permute-start = (bf16[64,1024]{1,0:T(8,128)(2,1)S(1)}, bf16[64,1024]{1,0:T(8,128)(2,1)}, u32[]{:S(2)}, u32[]{:S(2)}) collective-permute-start(bf16[64,1024]{1,0:T(8,128)(2,1)S(1)} %convolution_convert_fusion), channel_id=1, source_target_pairs={{248,0},{0,8},{8,16},{16,24},{24,32},{32,40},{40,48},{48,56},{56,6... | collective-permute-start | bytes 393224 | tf_op jit(solution)/shard_map/ppermute | solution.py:12
  13.5 60.3 %collective-permute-start.1 = (bf16[64,1024]{1,0:T(8,128)(2,1)S(1)}, bf16[64,1024]{1,0:T(8,128)(2,1)}, u32[]{:S(2)}, u32[]{:S(2)}) collective-permute-start(bf16[64,1024]{1,0:T(8,128)(2,1)S(1)} %convolution_convert_fusion), channel_id=1, source_target_pairs={{8,0},{16,8},{24,16},{32,24},{40,32},{48,40},{56,48},{64,56},{72,6... | collective-permute-start | bytes 393224 | tf_op jit(solution)/shard_map/ppermute | solution.py:12
  27.9 47.5 %all-to-all-start = ((bf16[64,32,128]{2,0,1:T(8,128)(2,1)}), bf16[64,32,128]{2,0,1:T(8,128)(2,1)}, u32[]{:S(2)}, u32[]{:S(2)}) async-start(bf16[64,32,128]{2,0,1:T(8,128)(2,1)} %bitcast.5), calls=%async_computation | async-start | bytes 1048576 | tf_op jit(solution)/shard_map/all_to_all | solution.py:53
  40.4 11.2 %copy-start.13 = (s32[12,4]{0,1:T(4,128)S(1)}, s32[12,4]{0,1:T(4,128)}, u32[]{:S(2)}) copy-start(s32[12,4]{0,1:T(4,128)} %param.13) | copy-start | bytes 580
  64.4 1.3 copy-start.4
  65.7 6.7 %copy-start.1 = (bf16[128,8,4,256]{3,1,2,0:T(8,128)(2,1)}, bf16[128,8,4,256]{3,1,2,0:T(8,128)(2,1)S(1)}, u32[]{:S(2)}) copy-start(bf16[128,8,4,256]{3,1,2,0:T(8,128)(2,1)S(1)} %copy.48) | copy-start | bytes 6291460
  65.7 2.0 copy-start.11
  70.1 3.7 copy-start.2
  75.4 3.1 copy-start.10
  78.5 23.1 %copy-start.7 = (bf16[64,1024]{0,1:T(8,128)(2,1)S(1)}, bf16[64,1024]{0,1:T(8,128)(2,1)}, u32[]{:S(2)}) copy-start(bf16[64,1024]{0,1:T(8,128)(2,1)} %copy.36) | copy-start | bytes 393220
  101.6 4.1 copy-start.3
  105.6 3.4 copy-start.9
  107.2 32.1 %collective-permute-start.2 = (f32[64,1024]{1,0:T(8,128)}, f32[64,1024]{1,0:T(8,128)}, u32[]{:S(2)}, u32[]{:S(2)}) collective-permute-start(f32[64,1024]{1,0:T(8,128)} %fusion.11), channel_id=1, source_target_pairs={{8,0},{16,8},{24,16},{32,24},{40,32},{48,40},{56,48},{64,56},{72,6... | collective-permute-start | bytes 786440 | tf_op jit(solution)/shard_map/ppermute | solution.py:12
  107.6 31.7 %collective-permute-start.3 = (f32[64,1024]{1,0:T(8,128)}, f32[64,1024]{1,0:T(8,128)}, u32[]{:S(2)}, u32[]{:S(2)}) collective-permute-start(f32[64,1024]{1,0:T(8,128)} %fusion.12), channel_id=1, source_target_pairs={{248,0},{0,8},{8,16},{16,24},{24,32},{32,40},{40,48},{48,56},{56,6... | collective-permute-start | bytes 786440 | tf_op jit(solution)/shard_map/ppermute | solution.py:12
  126.3 12.9 %copy-start.12 = (s32[1,32,128]{2,1,0:T(8,128)S(1)}, s32[1,32,128]{2,1,0:T(8,128)}, u32[]{:S(2)}) copy-start(s32[1,32,128]{2,1,0:T(8,128)} %param.14) | copy-start | bytes 49156
  126.3 13.0 %copy-start.5 = (bf16[128,8,4,256]{3,1,2,0:T(8,128)(2,1)S(1)}, bf16[128,8,4,256]{3,1,2,0:T(8,128)(2,1)}, u32[]{:S(2)}) copy-start(bf16[128,8,4,256]{3,1,2,0:T(8,128)(2,1)} %copy-done.4) | copy-start | bytes 6291460
  128.6 28.7 %all-to-all-start.1 = ((bf16[64,32,128]{2,0,1:T(8,128)(2,1)}), bf16[64,32,128]{2,0,1:T(8,128)(2,1)}, u32[]{:S(2)}, u32[]{:S(2)}) async-start(bf16[64,32,128]{2,0,1:T(8,128)(2,1)} %fusion.2), calls=%async_computation.1 | async-start | bytes 1048576 | tf_op jit(solution)/shard_map/all_to_all | solution.py:74
  139.2 118.0 %reduce-scatter.4.cloned.1.call-start = ((), (), s32[]{:S(2)}) async-start(), calls=%async_computation.4 | async-start | bytes 2359296
  160.4 22.9 %copy-start.8 = (bf16[512,64]{0,1:T(8,128)(2,1)S(1)}, bf16[512,64]{0,1:T(8,128)(2,1)}, u32[]{:S(2)}) copy-start(bf16[512,64]{0,1:T(8,128)(2,1)} %param.11) | copy-start | bytes 196612
  187.9 1.2 copy-start.6
  187.9 244.8 %all-reduce.2.cloned.1.call-start = ((), (), s32[]{:S(2)}) async-start(), calls=%async_computation.3 | async-start | bytes 262144 | tf_op jit(solution)/shard_map/psum | solution.py:81
Sparse Core Ops, SparseCore 0:
  188.0 36.5 reduce-scatter.3
Sparse Core Ops, SparseCore 1:
  191.6 241.1 all-reduce.1
where the time goes:
time: 443 us; the launch traced here: 442 us
  waiting for transfers between devices  188 us (42%)
  blocking collectives  67.3 us (15%)
  local copies, waits for them, and re-layouts  64.8 us (15%)
  other arithmetic  63.3 us (14%)
  starting transfers between devices  28.3 us (6%)
  between operations  15.8 us (4%)
  matrix products  14.3 us (3%)
    psum x1, waiting for transfers between devices, on_device(): weight_grad, bias_grad = lax.psum((weight_part, bias_part), 'dom')  174 us
    psum x1, blocking collectives, on_device(): weight_grad, bias_grad = lax.psum((weight_part, bias_part), 'dom')  67.3 us
    scatter-add x1, other arithmetic, on_device(): summed.at[:, recv_rows[0].reshape(-1)]  23.1 us
    scatter-add x1, other arithmetic, on_device(): map_grad.at[:, send_rows[0].reshape(-1)]  22.9 us
    gather x2, local copies, waits for them, and re-layouts, on_device(): pre_grad.astype(jnp.float32)[:, recv_rows[0]] * slot_weight[None]  17.3 us
    all_to_all x1, waiting for transfers between devices, on_device(): lax.all_to_all(message, 'dom', split_axis=1, concat_axis=1, tiled=True)  14.4 us
    unnamed x37, local copies, waits for them, and re-layouts  13.5 us
    gather x2, local copies, waits for them, and re-layouts, on_device(): outgoing = mapped[:, send_rows[0]]  13.2 us
  transfers between devices with their start and end apart: 8, of which 2 were waited for; matrix products, arithmetic and copies ran while one was open for 17% of the time, Pallas kernels for 0%

commit v1 on v0

v1 whole, which is shorter than its diff:
```python
import functools

import jax
import jax.numpy as jnp
from jax import lax
from jax.experimental import pallas as pl
from jax.experimental.pallas import tpu as pltpu
from jax.sharding import PartitionSpec as P

MESH = pl.DeviceIdType.MESH
F32 = jnp.float32
BF16 = jnp.bfloat16
TILE = 256
NT = (((1,), (1,)), ((), ()))
ZS = 8
CHIPS = 16
BLOCKS = 32
HIDS = 8


def dot(a, b):
    return jnp.dot(a, b, preferred_element_type=F32)


def dot_nt(a, b):
    return lax.dot_general(a, b, NT, preferred_element_type=F32)


def row_to_column(row, rows):
    lanes = row.shape[1]
    at = lax.broadcasted_iota(jnp.int32, (rows, lanes), 0)
    to = lax.broadcasted_iota(jnp.int32, (rows, lanes), 1)
    return jnp.sum(jnp.where(at == to, row, 0.0), axis=1, keepdims=True)


def kernel(
    wt_ref,
    feat_hbm,
    band_hbm,
    live_ref,
    send_ref,
    recv_ref,
    ew_ref,
    slots_ref,
    bias_ref,
    cot_hbm,
    out_ref,
    fg_ref,
    wg_ref,
    bg_ref,
    feat,
    band,
    cot,
    mapped,
    near,
    picks,
    puts,
    weights,
    acc,
    pre,
    term,
    term_in,
    out1,
    in1,
    out2,
    in2,
    wsend,
    wrecv,
    wfull,
    gb,
    bias_out,
    bias_in,
    pieces,
    pieces_in,
    summed,
    wg_all,
    load_sem,
    a1_send,
    a1_recv,
    n1_send,
    n1_recv,
    a2_send,
    a2_recv,
    n2_send,
    n2_recv,
    w_send,
    w_recv,
    b_send,
    b_recv,
    g_send,
    g_recv,
    rs_send,
    rs_recv,
    ag_send,
    ag_recv,
):
    me = lax.axis_index("dom")
    hid = lax.axis_index("hid")
    core = lax.rem(me, 2)
    z = lax.rem(me // 2, ZS)
    yh = me // (2 * ZS)
    left = lax.rem(me + BLOCKS - 1, BLOCKS)
    right = lax.rem(me + 1, BLOCKS)
    rows = mapped.shape[1]
    width = mapped.shape[0]

    def remote(src, dst, ssem, rsem, **where):
        return pltpu.make_async_remote_copy(
            src_ref=src, dst_ref=dst, send_sem=ssem, recv_sem=rsem,
            device_id=where, device_id_type=MESH,
        )

    def place(k):
        step = k // 2
        half = (step + 1) // 2
        dz = lax.rem(4 + half * (1 - 2 * lax.rem(step, 2)) + ZS, ZS)
        dy = 1 - lax.rem(k, 2)
        slot = 2 * dz + dy
        back = 2 * lax.rem(ZS - dz, ZS) + dy
        chip = lax.rem(yh + dy, 2) * ZS + lax.rem(z + dz, ZS)
        return slot, back, chip

    feat_copy = pltpu.make_async_copy(feat_hbm, feat, load_sem.at[0])
    band_copy = pltpu.make_async_copy(band_hbm, band, load_sem.at[1])
    cot_copy = pltpu.make_async_copy(cot_hbm, cot, load_sem.at[2])
    feat_copy.start()
    band_copy.start()
    cot_copy.start()

    barrier = pltpu.get_barrier_semaphore()

    @pl.loop(1, BLOCKS)
    def _(j):
        pl.semaphore_signal(barrier, inc=1, device_id={"dom": lax.rem(me + j, BLOCKS)}, device_id_type=MESH)

    @pl.loop(1, HIDS)
    def _(j):
        pl.semaphore_signal(barrier, inc=1, device_id={"hid": lax.rem(hid + j, HIDS)}, device_id_type=MESH)

    slot_ids = lax.broadcasted_iota(jnp.int32, (BLOCKS, 128), 1).astype(F32)
    counts = row_to_column(slots_ref[...].astype(F32), BLOCKS)
    weights[...] = jnp.where(slot_ids < counts, ew_ref[...], 0.0)
    wt = wt_ref[...]
    wsend[...] = jnp.zeros_like(wsend)
    for p in range(HIDS):
        wsend[p, :, :width] = wt[:, p * width:(p + 1) * width]
    wrecv[0] = wsend[hid]

    feat_copy.wait()

    @pl.loop(0, rows // TILE)
    def _(j):
        cols = pl.ds(pl.multiple_of(j * TILE, TILE), TILE)
        mapped[:, cols] = dot(wt_ref[...], feat[:, cols]).astype(BF16)

    pl.semaphore_wait(barrier, BLOCKS - 1 + HIDS - 1)

    to_right = remote(mapped, near.at[0], n1_send.at[0], n1_recv.at[0], dom=right)
    to_left = remote(mapped, near.at[1], n1_send.at[1], n1_recv.at[1], dom=left)
    to_right.start()
    to_left.start()

    def onehot(ref, chip):
        index = jnp.concatenate(
            [ref[pl.ds(2 * chip, 1), :], ref[pl.ds(2 * chip + 1, 1), :]], axis=1
        )
        at = lax.broadcasted_iota(jnp.int32, (rows, 2 * 128), 0)
        return jnp.where(at == index, 1.0, 0.0).astype(BF16)

    def slot_row(chip):
        return jnp.concatenate(
            [weights[pl.ds(2 * chip, 1), :], weights[pl.ds(2 * chip + 1, 1), :]], axis=1
        )

    def pick(slot, chip):
        picks[slot] = onehot(send_ref, chip)
        got = dot(mapped[...], picks[slot]).astype(BF16)
        out1[slot, 0] = got[:, :128]
        out1[slot, 1] = got[:, 128:]

    def ship(outs, ins, ssem, rsem, slot, back, chip, h):
        return remote(
            outs.at[slot, h], ins.at[back, core], ssem.at[slot, h], rsem.at[back, core],
            dom=2 * chip + h,
        )

    own = yh * ZS + z

    @pl.loop(0, CHIPS - 1)
    def _(k):
        slot, back, chip = place(k)
        pick(slot, chip)
        for h in range(2):
            ship(out1, in1, a1_send, a1_recv, slot, back, chip, h).start()

    pick(0, own)
    ship(out1, in1, a1_send, a1_recv, 0, 0, own, 1 - core).start()
    in1[0, core] = out1[0, core]

    @pl.loop(1, HIDS)
    def _(j):
        peer = lax.rem(hid + j, HIDS)
        remote(wsend.at[peer], wrecv.at[HIDS - j], w_send.at[j], w_recv.at[HIDS - j], hid=peer).start()

    band_copy.wait()

    def dense_forward(source, s):
        @pl.loop(0, rows // TILE)
        def _(j):
            cols = pl.ds(pl.multiple_of(j * TILE, TILE), TILE)
            parts = [
                (source[:, t * TILE:(t + 1) * TILE].astype(F32)
                 * live_ref[j, s * 4 + t].astype(F32)).astype(BF16)
                for t in range(rows // TILE)
            ]
            got = dot(jnp.concatenate(parts, axis=1), band[s * rows:(s + 1) * rows, cols])
            if s == 1:
                acc[:, cols] = got
            else:
                acc[:, cols] += got

    dense_forward(mapped, 1)

    @pl.loop(0, CHIPS)
    def _(k):
        slot, _, chip = place(k)
        puts[slot] = onehot(recv_ref, chip)

    to_right.wait_recv()
    dense_forward(near.at[0], 0)
    to_left.wait_recv()
    dense_forward(near.at[1], 2)

    def put(slot, chip):
        pair = jnp.concatenate([in1[slot, 0], in1[slot, 1]], axis=1).astype(F32)
        acc[...] += dot_nt((pair * slot_row(chip)).astype(BF16), puts[slot])

    remote(out1.at[0, 0], in1.at[0, 1 - core], a1_send.at[0, 0], a1_recv.at[0, 1 - core], dom=left).wait_recv()
    put(0, own)

    @pl.loop(0, CHIPS - 1)
    def _(k):
        slot, _, chip = place(k)
        for h in range(2):
            remote(out1.at[slot, h], in1.at[slot, h], a1_send.at[slot, h], a1_recv.at[slot, h], dom=left).wait_recv()
        put(slot, chip)

    cot_copy.wait()
    act = acc[...] + row_to_column(bias_ref[...], width)
    gate = 1.0 / (1.0 + jnp.exp(-act))
    out_ref[...] = (act * gate).astype(BF16)
    grad = (cot[...].astype(F32) * (gate * (1.0 + act * (1.0 - gate)))).astype(BF16)
    pre[...] = grad
    bias_col = jnp.sum(grad.astype(F32), axis=1, keepdims=True)
    diagonal = lax.broadcasted_iota(jnp.int32, (width, 128), 0) == lax.broadcasted_iota(jnp.int32, (width, 128), 1)
    bias_row = jnp.sum(jnp.where(diagonal, bias_col, 0.0), axis=0, keepdims=True)
    bias_out[0] = jnp.broadcast_to(bias_row, (8, 128))

    def bias_peer(step):
        bit = 1 << step
        return me + bit * (1 - 2 * lax.rem(me // bit, 2))

    def bias_copy(step):
        return remote(bias_out.at[step], bias_in.at[step], b_send.at[step], b_recv.at[step], dom=bias_peer(step))

    def bias_step(step):
        bias_copy(step).wait_recv()
        total = bias_out[step] + bias_in[step]
        bias_out[step + 1] = total
        if step < 4:
            bias_copy(step + 1).start()

    bias_copy(0).start()

    def message(slot, chip):
        got = (dot(pre[...], puts[slot]) * slot_row(chip)).astype(BF16)
        out2[slot, 0] = got[:, :128]
        out2[slot, 1] = got[:, 128:]

    def send_messages(lo, hi):
        @pl.loop(lo, hi)
        def _(k):
            slot, back, chip = place(k)
            message(slot, chip)
            for h in range(2):
                ship(out2, in2, a2_send, a2_recv, slot, back, chip, h).start()

    def dense_backward(target, s):
        @pl.loop(0, rows // TILE)
        def _(t):
            cols = pl.ds(pl.multiple_of(t * TILE, TILE), TILE)
            parts = [
                (pre[:, j * TILE:(j + 1) * TILE].astype(F32)
                 * live_ref[j, s * 4 + t].astype(F32)).astype(BF16)
                for j in range(rows // TILE)
            ]
            band_rows = pl.ds(pl.multiple_of(s * rows + t * TILE, TILE), TILE)
            got = dot_nt(jnp.concatenate(parts, axis=1), band[band_rows, :])
            target[:, cols] = got.astype(target.dtype)

    send_messages(0, 6)
    dense_backward(term.at[0], 0)
    grad_left = remote(term.at[0], term_in.at[0], n2_send.at[0], n2_recv.at[0], dom=left)
    grad_left.start()
    dense_backward(term.at[1], 2)
    grad_right = remote(term.at[1], term_in.at[1], n2_send.at[1], n2_recv.at[1], dom=right)
    grad_right.start()
    send_messages(6, CHIPS - 1)
    message(0, own)
    ship(out2, in2, a2_send, a2_recv, 0, 0, own, 1 - core).start()
    in2[0, core] = out2[0, core]
    bias_step(0)

    dense_backward(acc, 1)

    @pl.loop(1, HIDS)
    def _(j):
        remote(wsend.at[j], wrecv.at[j], w_send.at[j], w_recv.at[j], dom=left).wait_recv()

    wfull[...] = jnp.transpose(
        wrecv[...].reshape(HIDS * width, 128).astype(F32), (1, 0)
    )[:width].astype(BF16)

    grad_left.wait_recv()
    grad_right.wait_recv()
    acc[...] += term_in[0].astype(F32) + term_in[1].astype(F32)

    def give_back(slot):
        pair = jnp.concatenate([in2[slot, 0], in2[slot, 1]], axis=1)
        acc[...] += dot_nt(pair, picks[slot])

    remote(out2.at[0, 0], in2.at[0, 1 - core], a2_send.at[0, 0], a2_recv.at[0, 1 - core], dom=left).wait_recv()
    give_back(0)

    @pl.loop(0, CHIPS - 1)
    def _(k):
        slot, _, chip = place(k)
        for h in range(2):
            remote(out2.at[slot, h], in2.at[slot, h], a2_send.at[slot, h], a2_recv.at[slot, h], dom=left).wait_recv()
        give_back(slot)

    gb[0] = acc[...].astype(BF16)

    @pl.loop(1, HIDS)
    def _(j):
        remote(gb.at[0], gb.at[HIDS - j], g_send.at[j], g_recv.at[HIDS - j], hid=lax.rem(hid + j, HIDS)).start()

    wg = dot_nt(gb[0], feat[...])
    for d in range(BLOCKS):
        r, c = d // 4, d % 4
        pieces[d] = wg[8 * r:8 * r + 8, 128 * c:128 * c + 128]

    @pl.loop(1, BLOCKS)
    def _(j):
        peer = lax.rem(me + j, BLOCKS)
        remote(pieces.at[peer], pieces_in.at[BLOCKS - j], rs_send.at[j], rs_recv.at[BLOCKS - j], dom=peer).start()

    bias_step(1)
    bias_step(2)

    summed[...] = pieces[me]

    @pl.loop(1, BLOCKS)
    def _(j):
        remote(pieces.at[j], pieces_in.at[j], rs_send.at[j], rs_recv.at[j], dom=left).wait_recv()
        summed[...] += pieces_in[j]

    @pl.loop(1, BLOCKS)
    def _(j):
        peer = lax.rem(me + j, BLOCKS)
        remote(summed, wg_all.at[me], ag_send.at[j], ag_recv.at[BLOCKS - j], dom=peer).start()

    wg_all[me] = summed[...]
    bias_step(3)
    bias_step(4)
    bg_ref[...] = bias_out[5, 0:1, :width]

    @pl.loop(1, HIDS)
    def _(j):
        remote(gb.at[0], gb.at[j], g_send.at[j], g_recv.at[j], dom=left).wait_recv()

    @pl.loop(0, rows // TILE)
    def _(j):
        cols = pl.ds(pl.multiple_of(j * TILE, TILE), TILE)
        stack = gb[:, :, cols].reshape(HIDS * width, TILE)
        fg_ref[:, cols] = dot(wfull[...], stack).astype(BF16)

    @pl.loop(1, BLOCKS)
    def _(j):
        remote(summed, wg_all.at[lax.rem(me + j, BLOCKS)], ag_send.at[j], ag_recv.at[j], dom=left).wait_recv()

    for d in range(BLOCKS):
        r, c = d // 4, d % 4
        wg_ref[8 * r:8 * r + 8, 128 * c:128 * c + 128] = wg_all[d]

    to_right.wait_send()
    to_left.wait_send()
    grad_left.wait_send()
    grad_right.wait_send()
    for step in range(5):
        bias_copy(step).wait_send()

    @pl.loop(0, CHIPS - 1)
    def _(k):
        slot, back, chip = place(k)
        for h in range(2):
            ship(out1, in1, a1_send, a1_recv, slot, back, chip, h).wait_send()
            ship(out2, in2, a2_send, a2_recv, slot, back, chip, h).wait_send()

    ship(out1, in1, a1_send, a1_recv, 0, 0, own, 1 - core).wait_send()
    ship(out2, in2, a2_send, a2_recv, 0, 0, own, 1 - core).wait_send()

    @pl.loop(1, HIDS)
    def _(j):
        peer = lax.rem(hid + j, HIDS)
        remote(wsend.at[peer], wrecv.at[HIDS - j], w_send.at[j], w_recv.at[HIDS - j], hid=peer).wait_send()
        remote(gb.at[0], gb.at[HIDS - j], g_send.at[j], g_recv.at[HIDS - j], hid=peer).wait_send()

    @pl.loop(1, BLOCKS)
    def _(j):
        peer = lax.rem(me + j, BLOCKS)
        remote(pieces.at[peer], pieces_in.at[BLOCKS - j], rs_send.at[j], rs_recv.at[BLOCKS - j], dom=peer).wait_send()
        remote(summed, wg_all.at[me], ag_send.at[j], ag_recv.at[BLOCKS - j], dom=peer).wait_send()


def on_device(
    features,
    weight,
    band_tiles,
    tile_live,
    send_rows,
    recv_rows,
    edge_weight,
    live_slots,
    bias_terms,
    cotangent,
):
    depth, rows = features.shape
    width = weight.shape[1]
    vmem = pl.BlockSpec(memory_space=pltpu.VMEM)
    hbm = pl.BlockSpec(memory_space=pl.ANY)
    smem = pl.BlockSpec(memory_space=pltpu.SMEM)
    dma = pltpu.SemaphoreType.DMA
    block = pltpu.VMEM((width, rows), BF16)
    lists = pltpu.VMEM((CHIPS, 2, width, 128), BF16)
    output, feature_grad, wg, bg = pl.pallas_call(
        kernel,
        out_shape=(
            jax.ShapeDtypeStruct((width, rows), BF16),
            jax.ShapeDtypeStruct((width, rows), BF16),
            jax.ShapeDtypeStruct((width, depth), F32),
            jax.ShapeDtypeStruct((1, width), F32),
        ),
        in_specs=[vmem, hbm, hbm, smem, vmem, vmem, vmem, vmem, vmem, hbm],
        out_specs=(vmem,) * 4,
        scratch_shapes=[
            pltpu.VMEM((depth, rows), BF16),
            pltpu.VMEM((3 * rows, rows), BF16),
            block,
            block,
            pltpu.VMEM((2, width, rows), BF16),
            pltpu.VMEM((CHIPS, rows, 256), BF16),
            pltpu.VMEM((CHIPS, rows, 256), BF16),
            pltpu.VMEM((BLOCKS, 128), F32),
            pltpu.VMEM((width, rows), F32),
            block,
            pltpu.VMEM((2, width, rows), BF16),
            pltpu.VMEM((2, width, rows), BF16),
            lists,
            lists,
            lists,
            lists,
            pltpu.VMEM((HIDS, width, 128), BF16),
            pltpu.VMEM((HIDS, width, 128), BF16),
            pltpu.VMEM((width, HIDS * width), BF16),
            pltpu.VMEM((HIDS, width, rows), BF16),
            pltpu.VMEM((6, 8, 128), F32),
            pltpu.VMEM((5, 8, 128), F32),
            pltpu.VMEM((BLOCKS, 8, 128), F32),
            pltpu.VMEM((BLOCKS, 8, 128), F32),
            pltpu.VMEM((8, 128), F32),
            pltpu.VMEM((BLOCKS, 8, 128), F32),
            dma((3,)),
            dma((CHIPS, 2)),
            dma((CHIPS, 2)),
            dma((2,)),
            dma((2,)),
            dma((CHIPS, 2)),
            dma((CHIPS, 2)),
            dma((2,)),
            dma((2,)),
            dma((HIDS,)),
            dma((HIDS,)),
            dma((5,)),
            dma((5,)),
            dma((HIDS,)),
            dma((HIDS,)),
            dma((BLOCKS,)),
            dma((BLOCKS,)),
            dma((BLOCKS,)),
            dma((BLOCKS,)),
        ],
        compiler_params=pltpu.CompilerParams(
            collective_id=0, has_side_effects=True, vmem_limit_bytes=56 << 20
        ),
    )(
        weight.T,
        features,
        band_tiles,
        tile_live.T,
        send_rows[0],
        recv_rows[0],
        edge_weight[0],
        live_slots,
        bias_terms.reshape(1, width),
        cotangent,
    )
    return (output, feature_grad, wg.T, bg.reshape(width))


def solution(mesh):
    return jax.shard_map(
        on_device,
        mesh=mesh,
        in_specs=(
            P(None, "dom"),
            P(None, "hid"),
            P(None, "dom"),
            P(None, "dom"),
            P("dom", None, None),
            P("dom", None, None),
            P("dom", None, None),
            P("dom", None),
            P("hid"),
            P("hid", "dom"),
        ),
        out_specs=(P("hid", "dom"), P("hid", "dom"), P(None, "hid"), P("hid")),
        check_vma=False,
    )
```

time: 443 us -> 81.9 us (0.18)
  waiting for transfers between devices: 188 us -> 0 us
  Pallas kernels: 0 us -> 75.2 us
  blocking collectives: 67.3 us -> 0 us
  other arithmetic: 63.3 us -> 0 us
  local copies, waits for them, and re-layouts: 64.8 us -> 5.82 us
  starting transfers between devices: 28.3 us -> 0 us
  between operations: 15.8 us -> 0.64 us
  matrix products: 14.3 us -> 0 us
    psum x1 -> x0, waiting for transfers between devices: 174 us -> none  [on_device(): weight_grad, bias_grad = lax.psum((weight_part, bias_part), 'dom')]
    pallas_call x0 -> x1, Pallas kernels: none -> 75.2 us  [on_device(): pl.pallas_call(kernel, out_shape=(jax.ShapeDtypeStruct((width, rows), BF1...]
    psum x1 -> x0, blocking collectives: 67.3 us -> none  [on_device(): weight_grad, bias_grad = lax.psum((weight_part, bias_part), 'dom')]
    scatter-add x2 -> x0, other arithmetic: 45.9 us -> none  [the longest x1 23.1 us: on_device(): summed.at[:, recv_rows[0].reshape(-1)]]
    gather x4 -> x0, local copies, waits for them, and re-layouts: 30.5 us -> none  [the longest x2 17.3 us: on_device(): pre_grad.astype(jnp.float32)[:, recv_rows[0]] * slot_weight[None]]
    all_to_all x2 -> x0, starting transfers between devices: 23 us -> none  [the longest x1 12.5 us: on_device(): lax.all_to_all(outgoing, 'dom', split_axis=1, concat_axis=1, tiled=True)]
    reshape x3 -> x0, local copies, waits for them, and re-layouts: 15.1 us -> none  [the longest x1 11.2 us: on_device(): band_tiles.reshape(3 * row_count // TILE, TILE, row_count // TILE, TILE)]
    all_to_all x2 -> x0, waiting for transfers between devices: 14.4 us -> none  [the longest x1 14.4 us: on_device(): lax.all_to_all(message, 'dom', split_axis=1, concat_axis=1, tiled=True)]
  transfers between devices with their start and end apart: 8 -> 0, of which waited for: 2 -> 0; matrix products, arithmetic and copies ran while one was open for 17% -> 0% of each run, Pallas kernels for 0% -> 0%
where the time goes in v1:
time: 81.9 us; the launch traced here: 81.7 us
  Pallas kernels  75.2 us (92%)
  local copies, waits for them, and re-layouts  5.82 us (7%)
    pallas_call x1, Pallas kernels, on_device(): pl.pallas_call(kernel, out_shape=(jax.ShapeDtypeStruct((width, rows), BF1...  75.2 us
    unnamed x4, local copies, waits for them, and re-layouts  5.82 us

profile of v1, /device:TPU:1, one launch (start us, length us, event | category | flops | bytes accessed | tf_op | source)
XLA Modules:
  0.0 81.7 jit_solution(6762373237912896209)
XLA Ops:
  0.6 75.2 %shard_map.129 = (bf16[64,1024]{1,0:T(8,128)(2,1)}, bf16[64,1024]{1,0:T(8,128)(2,1)}, f32[64,512]{1,0:T(8,128)}, f32[1,64]{1,0:T(1,128)}) custom-call(bf16[64,512]{1,0:T(8,128)(2,1)} %bitcast.9, bf16[512,1024]{1,0:T(8,128)(2,1)} %feat_hbm.1, bf16[3072,1024]{1,0:T(8,128)(2,1)} %band_hbm.1, s32[4,12]{1,0:T(4,128)} %bitcast.13, s32[32,128]{1,0:T(8,128)} %bitcast.10, ...), custom_call_target="tpu_custom_call" | custom-call | tf_op jit(solution)/shard_map/pallas_call | solution.py:446
  75.9 1.6 %copy.18 = bf16[64,1024]{1,0:T(8,128)(2,1)} copy(bf16[64,1024]{1,0:T(8,128)(2,1)} %get-tuple-element.16) | data formatting | bytes 262144
  77.5 1.6 %copy.19 = bf16[64,1024]{1,0:T(8,128)(2,1)} copy(bf16[64,1024]{1,0:T(8,128)(2,1)} %get-tuple-element.17) | data formatting | bytes 262144
  79.0 1.6 %copy.20 = f32[512,64]{0,1:T(8,128)} copy(f32[512,64]{0,1:T(8,128)} %bitcast.8) | data formatting | bytes 262144
  80.6 1.1 %copy.21 = f32[64]{0:T(128)} copy(f32[64]{0:T(128)} %bitcast.15) | data formatting | bytes 512

commit v2 on v1

v2 whole, which is shorter than its diff:
```python
import jax
import jax.numpy as jnp
from jax import lax
from jax.experimental import pallas as pl
from jax.experimental.pallas import tpu as pltpu
from jax.sharding import PartitionSpec as P

MESH = pl.DeviceIdType.MESH
F32 = jnp.float32
BF16 = jnp.bfloat16
TILE = 256
NT = (((1,), (1,)), ((), ()))
ZS = 8
CHIPS = 16
BLOCKS = 32
HIDS = 8


def dot(a, b):
    return jnp.dot(a, b, preferred_element_type=F32)


def dot_nt(a, b):
    return lax.dot_general(a, b, NT, preferred_element_type=F32)


def row_to_column(row, rows):
    lanes = row.shape[1]
    at = lax.broadcasted_iota(jnp.int32, (rows, lanes), 0)
    to = lax.broadcasted_iota(jnp.int32, (rows, lanes), 1)
    return jnp.sum(jnp.where(at == to, row, 0.0), axis=1, keepdims=True)


def kernel(
    wt_hbm,
    feat_hbm,
    band_hbm,
    live_hbm,
    send_hbm,
    recv_hbm,
    ew_hbm,
    slots_hbm,
    bias_hbm,
    cot_hbm,
    out_ref,
    fg_ref,
    wg_ref,
    bg_ref,
    wt_ref,
    feat,
    band,
    live_ref,
    send_ref,
    recv_ref,
    ew_ref,
    slots_ref,
    bias_ref,
    cot,
    mapped,
    near,
    picks,
    puts,
    weights,
    acc,
    pre,
    term,
    term_in,
    out1,
    in1,
    out2,
    in2,
    wsend,
    wrecv,
    wfull,
    gb,
    bias_out,
    bias_in,
    pieces,
    pieces_in,
    summed,
    wg_all,
    load_sem,
    a1_send,
    a1_recv,
    n1_send,
    n1_recv,
    a2_send,
    a2_recv,
    n2_send,
    n2_recv,
    w_send,
    w_recv,
    b_send,
    b_recv,
    g_send,
    g_recv,
    rs_send,
    rs_recv,
    ag_send,
    ag_recv,
):
    me = lax.axis_index("dom")
    hid = lax.axis_index("hid")
    core = lax.rem(me, 2)
    z = lax.rem(me // 2, ZS)
    yh = me // (2 * ZS)
    own = yh * ZS + z
    left = lax.rem(me + BLOCKS - 1, BLOCKS)
    right = lax.rem(me + 1, BLOCKS)
    rows = mapped.shape[1]
    width = mapped.shape[0]
    half = width // 2
    barrier = pltpu.get_barrier_semaphore()

    @pl.loop(1, BLOCKS)
    def _(j):
        pl.semaphore_signal(barrier, inc=1, device_id={"dom": lax.rem(me + j, BLOCKS)}, device_id_type=MESH)

    @pl.loop(1, HIDS)
    def _(j):
        pl.semaphore_signal(barrier, inc=1, device_id={"hid": lax.rem(hid + j, HIDS)}, device_id_type=MESH)

    loads = [
        pltpu.make_async_copy(src, dst, load_sem.at[i])
        for i, (src, dst) in enumerate((
            (wt_hbm, wt_ref), (feat_hbm, feat), (send_hbm, send_ref), (slots_hbm, slots_ref),
            (ew_hbm, ew_ref), (recv_hbm, recv_ref), (bias_hbm, bias_ref), (live_hbm, live_ref),
            (band_hbm, band), (cot_hbm, cot),
        ))
    ]
    for load in loads:
        load.start()

    def remote(src, dst, ssem, rsem, **where):
        return pltpu.make_async_remote_copy(
            src_ref=src, dst_ref=dst, send_sem=ssem, recv_sem=rsem,
            device_id=where, device_id_type=MESH,
        )

    def place(k):
        step = k // 2
        far = (step + 1) // 2
        dz = lax.rem(4 + far * (1 - 2 * lax.rem(step, 2)) + ZS, ZS)
        dy = 1 - lax.rem(k, 2)
        slot = 2 * dz + dy
        back = 2 * lax.rem(ZS - dz, ZS) + dy
        chip = lax.rem(yh + dy, 2) * ZS + lax.rem(z + dz, ZS)
        return slot, back, chip

    for load in loads[:4]:
        load.wait()

    @pl.loop(0, rows // TILE)
    def _(j):
        cols = pl.ds(pl.multiple_of(j * TILE, TILE), TILE)
        mapped[:, cols] = dot(wt_ref[...], feat[:, cols]).astype(BF16)

    pl.semaphore_wait(barrier, BLOCKS - 1 + HIDS - 1)

    to_right = remote(mapped, near.at[0], n1_send.at[0], n1_recv.at[0], dom=right)
    to_left = remote(mapped, near.at[1], n1_send.at[1], n1_recv.at[1], dom=left)
    to_right.start()
    to_left.start()

    def onehot(ref, chip):
        index = jnp.concatenate(
            [ref[pl.ds(2 * chip, 1), :], ref[pl.ds(2 * chip + 1, 1), :]], axis=1
        )
        at = lax.broadcasted_iota(jnp.int32, (rows, 2 * 128), 0)
        return jnp.where(at == index, 1.0, 0.0).astype(BF16)

    def slot_row(chip):
        return jnp.concatenate(
            [weights[pl.ds(2 * chip, 1), :], weights[pl.ds(2 * chip + 1, 1), :]], axis=1
        )

    def pick(slot, chip):
        picks[slot] = onehot(send_ref, chip)
        got = dot(mapped[...], picks[slot]).astype(BF16)
        for h in range(2):
            for c in range(2):
                out1[h, slot, c] = got[h * half:(h + 1) * half, c * 128:(c + 1) * 128]

    def ship(first, h, slot, back, chip, c):
        outs, ins, ssem, rsem = (out1, in1, a1_send, a1_recv) if first else (out2, in2, a2_send, a2_recv)
        return remote(
            outs.at[h, slot, c], ins.at[h, back, core], ssem.at[h, slot, c], rsem.at[h, back, core],
            dom=2 * chip + c,
        )

    def arrive(first, h, slot, c):
        outs, ins, ssem, rsem = (out1, in1, a1_send, a1_recv) if first else (out2, in2, a2_send, a2_recv)
        remote(
            outs.at[h, slot, c], ins.at[h, slot, c], ssem.at[h, slot, c], rsem.at[h, slot, c], dom=left
        ).wait_recv()

    @pl.loop(0, CHIPS - 1)
    def _(k):
        slot, back, chip = place(k)
        pick(slot, chip)
        for c in range(2):
            ship(True, 0, slot, back, chip, c).start()

    pick(0, own)
    for h in range(2):
        ship(True, h, 0, 0, own, 1 - core).start()
        in1[h, 0, core] = out1[h, 0, core]

    @pl.loop(0, CHIPS - 1)
    def _(k):
        slot, back, chip = place(k)
        for c in range(2):
            ship(True, 1, slot, back, chip, c).start()

    for load in loads[4:]:
        load.wait()

    wt = wt_ref[...]
    wsend[...] = jnp.zeros_like(wsend)
    for p in range(HIDS):
        wsend[p, :, :width] = wt[:, p * width:(p + 1) * width]
    wrecv[0] = wsend[hid]

    @pl.loop(1, HIDS)
    def _(j):
        peer = lax.rem(hid + j, HIDS)
        remote(wsend.at[peer], wrecv.at[HIDS - j], w_send.at[j], w_recv.at[HIDS - j], hid=peer).start()

    slot_ids = lax.broadcasted_iota(jnp.int32, (BLOCKS, 128), 1).astype(F32)
    counts = row_to_column(slots_ref[...].astype(F32), BLOCKS)
    weights[...] = jnp.where(slot_ids < counts, ew_ref[...], 0.0)

    def dense_forward(source, s):
        @pl.loop(0, rows // TILE)
        def _(j):
            cols = pl.ds(pl.multiple_of(j * TILE, TILE), TILE)
            parts = [
                (source[:, t * TILE:(t + 1) * TILE].astype(F32)
                 * live_ref[j, s * 4 + t].astype(F32)).astype(BF16)
                for t in range(rows // TILE)
            ]
            got = dot(jnp.concatenate(parts, axis=1), band[s * rows:(s + 1) * rows, cols])
            if s == 1:
                acc[:, cols] = got
            else:
                acc[:, cols] += got

    dense_forward(mapped, 1)

    @pl.loop(0, CHIPS)
    def _(k):
        slot, _, chip = place(k)
        puts[slot] = onehot(recv_ref, chip)

    to_right.wait_recv()
    dense_forward(near.at[0], 0)
    to_left.wait_recv()
    dense_forward(near.at[1], 2)

    bias_in_col = row_to_column(bias_ref[...], width)

    def put(h, slot, chip):
        pair = jnp.concatenate([in1[h, slot, 0], in1[h, slot, 1]], axis=1).astype(F32)
        acc[h * half:(h + 1) * half] += dot_nt((pair * slot_row(chip)).astype(BF16), puts[slot])

    def activate(h):
        part = slice(h * half, (h + 1) * half)
        arrive(True, h, 0, 1 - core)
        put(h, 0, own)

        @pl.loop(0, CHIPS - 1)
        def _(k):
            slot, _, chip = place(k)
            for c in range(2):
                arrive(True, h, slot, c)
            put(h, slot, chip)

        act = acc[part] + bias_in_col[part]
        gate = 1.0 / (1.0 + jnp.exp(-act))
        out_ref[part] = (act * gate).astype(BF16)
        pre[part] = (cot[part].astype(F32) * (gate * (1.0 + act * (1.0 - gate)))).astype(BF16)

    def message(h, slot, chip):
        got = (dot(pre[h * half:(h + 1) * half], puts[slot]) * slot_row(chip)).astype(BF16)
        out2[h, slot, 0] = got[:, :128]
        out2[h, slot, 1] = got[:, 128:]

    def send_messages(h):
        @pl.loop(0, CHIPS - 1)
        def _(k):
            slot, back, chip = place(k)
            message(h, slot, chip)
            for c in range(2):
                ship(False, h, slot, back, chip, c).start()

        message(h, 0, own)
        ship(False, h, 0, 0, own, 1 - core).start()
        in2[h, 0, core] = out2[h, 0, core]

    def dense_backward(target, s):
        @pl.loop(0, rows // TILE)
        def _(t):
            cols = pl.ds(pl.multiple_of(t * TILE, TILE), TILE)
            parts = [
                (pre[:, j * TILE:(j + 1) * TILE].astype(F32)
                 * live_ref[j, s * 4 + t].astype(F32)).astype(BF16)
                for j in range(rows // TILE)
            ]
            band_rows = pl.ds(pl.multiple_of(s * rows + t * TILE, TILE), TILE)
            got = dot_nt(jnp.concatenate(parts, axis=1), band[band_rows, :])
            target[:, cols] = got.astype(target.dtype)

    def bias_copy(step):
        bit = 1 << step
        peer = me + bit * (1 - 2 * lax.rem(me // bit, 2))
        return remote(bias_out.at[step], bias_in.at[step], b_send.at[step], b_recv.at[step], dom=peer)

    def bias_step(step):
        bias_copy(step).wait_recv()
        bias_out[step + 1] = bias_out[step] + bias_in[step]
        if step < 4:
            bias_copy(step + 1).start()

    activate(0)
    send_messages(0)
    activate(1)

    dense_backward(term.at[0], 0)
    grad_left = remote(term.at[0], term_in.at[0], n2_send.at[0], n2_recv.at[0], dom=left)
    grad_left.start()
    dense_backward(term.at[1], 2)
    grad_right = remote(term.at[1], term_in.at[1], n2_send.at[1], n2_recv.at[1], dom=right)
    grad_right.start()
    bias_col = jnp.sum(pre[...].astype(F32), axis=1, keepdims=True)
    diagonal = lax.broadcasted_iota(jnp.int32, (width, 128), 0) == lax.broadcasted_iota(jnp.int32, (width, 128), 1)
    bias_row = jnp.sum(jnp.where(diagonal, bias_col, 0.0), axis=0, keepdims=True)
    bias_out[0] = jnp.broadcast_to(bias_row, (8, 128))
    bias_copy(0).start()
    send_messages(1)
    bias_step(0)

    dense_backward(acc, 1)

    @pl.loop(1, HIDS)
    def _(j):
        remote(wsend.at[j], wrecv.at[j], w_send.at[j], w_recv.at[j], dom=left).wait_recv()

    wfull[...] = jnp.transpose(
        wrecv[...].reshape(HIDS * width, 128).astype(F32), (1, 0)
    )[:width].astype(BF16)

    grad_left.wait_recv()
    grad_right.wait_recv()
    acc[...] += term_in[0].astype(F32) + term_in[1].astype(F32)

    def give_back(h, slot):
        pair = jnp.concatenate([in2[h, slot, 0], in2[h, slot, 1]], axis=1)
        acc[h * half:(h + 1) * half] += dot_nt(pair, picks[slot])

    def gradient(h):
        arrive(False, h, 0, 1 - core)
        give_back(h, 0)

        @pl.loop(0, CHIPS - 1)
        def _(k):
            slot, _, chip = place(k)
            for c in range(2):
                arrive(False, h, slot, c)
            give_back(h, slot)

        part = slice(h * half, (h + 1) * half)
        gb[0, part] = acc[part].astype(BF16)

    def share(h, j):
        part = pl.ds(h * half, half)
        return remote(
            gb.at[0, part], gb.at[HIDS - j, part], g_send.at[h, j], g_recv.at[h, HIDS - j],
            hid=lax.rem(hid + j, HIDS),
        )

    def share_all(h):
        @pl.loop(1, HIDS)
        def _(j):
            share(h, j).start()

    gradient(0)
    share_all(0)
    gradient(1)

    wg = dot_nt(gb[0], feat[...])
    for d in range(BLOCKS):
        r, c = d // 4, d % 4
        pieces[d] = wg[8 * r:8 * r + 8, 128 * c:128 * c + 128]

    @pl.loop(1, BLOCKS)
    def _(j):
        peer = lax.rem(me + j, BLOCKS)
        remote(pieces.at[peer], pieces_in.at[BLOCKS - j], rs_send.at[j], rs_recv.at[BLOCKS - j], dom=peer).start()

    share_all(1)
    bias_step(1)
    summed[...] = pieces[me]

    @pl.loop(1, BLOCKS)
    def _(j):
        remote(pieces.at[j], pieces_in.at[j], rs_send.at[j], rs_recv.at[j], dom=left).wait_recv()
        summed[...] += pieces_in[j]

    @pl.loop(1, BLOCKS)
    def _(j):
        peer = lax.rem(me + j, BLOCKS)
        remote(summed, wg_all.at[me], ag_send.at[j], ag_recv.at[BLOCKS - j], dom=peer).start()

    wg_all[me] = summed[...]
    bias_step(2)
    bias_step(3)

    for h in range(2):
        @pl.loop(1, HIDS)
        def _(j):
            part = pl.ds(h * half, half)
            remote(gb.at[0, part], gb.at[j, part], g_send.at[h, j], g_recv.at[h, j], dom=left).wait_recv()

    @pl.loop(0, rows // TILE)
    def _(j):
        cols = pl.ds(pl.multiple_of(j * TILE, TILE), TILE)
        stack = gb[:, :, cols].reshape(HIDS * width, TILE)
        fg_ref[:, cols] = dot(wfull[...], stack).astype(BF16)

    bias_step(4)
    bg_ref[...] = bias_out[5, 0:1, :width]

    @pl.loop(1, BLOCKS)
    def _(j):
        remote(summed, wg_all.at[lax.rem(me + j, BLOCKS)], ag_send.at[j], ag_recv.at[j], dom=left).wait_recv()

    for d in range(BLOCKS):
        r, c = d // 4, d % 4
        wg_ref[8 * r:8 * r + 8, 128 * c:128 * c + 128] = wg_all[d]

    to_right.wait_send()
    to_left.wait_send()
    grad_left.wait_send()
    grad_right.wait_send()
    for step in range(5):
        bias_copy(step).wait_send()

    @pl.loop(0, CHIPS - 1)
    def _(k):
        slot, back, chip = place(k)
        for h in range(2):
            for c in range(2):
                ship(True, h, slot, back, chip, c).wait_send()
                ship(False, h, slot, back, chip, c).wait_send()

    for h in range(2):
        ship(True, h, 0, 0, own, 1 - core).wait_send()
        ship(False, h, 0, 0, own, 1 - core).wait_send()

    @pl.loop(1, HIDS)
    def _(j):
        peer = lax.rem(hid + j, HIDS)
        remote(wsend.at[peer], wrecv.at[HIDS - j], w_send.at[j], w_recv.at[HIDS - j], hid=peer).wait_send()
        for h in range(2):
            share(h, j).wait_send()

    @pl.loop(1, BLOCKS)
    def _(j):
        peer = lax.rem(me + j, BLOCKS)
        remote(pieces.at[peer], pieces_in.at[BLOCKS - j], rs_send.at[j], rs_recv.at[BLOCKS - j], dom=peer).wait_send()
        remote(summed, wg_all.at[me], ag_send.at[j], ag_recv.at[BLOCKS - j], dom=peer).wait_send()


def finish(*refs):
    sources, targets, sem = refs[:4], refs[4:8], refs[8]
    copies = [
        pltpu.make_async_copy(src, dst, sem.at[i])
        for i, (src, dst) in enumerate(zip(sources, targets))
    ]
    for copy in copies:
        copy.start()
    for copy in copies:
        copy.wait()


def on_device(
    features,
    weight,
    band_tiles,
    tile_live,
    send_rows,
    recv_rows,
    edge_weight,
    live_slots,
    bias_terms,
    cotangent,
):
    depth, rows = features.shape
    width = weight.shape[1]
    vmem = pl.BlockSpec(memory_space=pltpu.VMEM)
    hbm = pl.BlockSpec(memory_space=pltpu.HBM)
    dma = pltpu.SemaphoreType.DMA
    block = pltpu.VMEM((width, rows), BF16)
    lists = pltpu.VMEM((2, CHIPS, 2, width // 2, 128), BF16)
    results = (((width, rows), BF16), ((width, rows), BF16), ((width, depth), F32), ((1, width), F32))
    parts = pl.pallas_call(
        kernel,
        out_shape=tuple(pltpu.VMEM(*r) for r in results),
        in_specs=[hbm] * 10,
        out_specs=(vmem,) * 4,
        scratch_shapes=[
            pltpu.VMEM((width, depth), BF16),
            pltpu.VMEM((depth, rows), BF16),
            pltpu.VMEM((3 * rows, rows), BF16),
            pltpu.SMEM((4, 12), jnp.int32),
            pltpu.VMEM((BLOCKS, 128), jnp.int32),
            pltpu.VMEM((BLOCKS, 128), jnp.int32),
            pltpu.VMEM((BLOCKS, 128), F32),
            pltpu.VMEM((1, BLOCKS), jnp.int32),
            pltpu.VMEM((1, width), F32),
            block,
            block,
            pltpu.VMEM((2, width, rows), BF16),
            pltpu.VMEM((CHIPS, rows, 256), BF16),
            pltpu.VMEM((CHIPS, rows, 256), BF16),
            pltpu.VMEM((BLOCKS, 128), F32),
            pltpu.VMEM((width, rows), F32),
            block,
            pltpu.VMEM((2, width, rows), BF16),
            pltpu.VMEM((2, width, rows), BF16),
            lists,
            lists,
            lists,
            lists,
            pltpu.VMEM((HIDS, width, 128), BF16),
            pltpu.VMEM((HIDS, width, 128), BF16),
            pltpu.VMEM((width, HIDS * width), BF16),
            pltpu.VMEM((HIDS, width, rows), BF16),
            pltpu.VMEM((6, 8, 128), F32),
            pltpu.VMEM((5, 8, 128), F32),
            pltpu.VMEM((BLOCKS, 8, 128), F32),
            pltpu.VMEM((BLOCKS, 8, 128), F32),
            pltpu.VMEM((8, 128), F32),
            pltpu.VMEM((BLOCKS, 8, 128), F32),
            dma((10,)),
            dma((2, CHIPS, 2)),
            dma((2, CHIPS, 2)),
            dma((2,)),
            dma((2,)),
            dma((2, CHIPS, 2)),
            dma((2, CHIPS, 2)),
            dma((2,)),
            dma((2,)),
            dma((HIDS,)),
            dma((HIDS,)),
            dma((5,)),
            dma((5,)),
            dma((2, HIDS)),
            dma((2, HIDS)),
            dma((BLOCKS,)),
            dma((BLOCKS,)),
            dma((BLOCKS,)),
            dma((BLOCKS,)),
        ],
        compiler_params=pltpu.CompilerParams(
            collective_id=0, has_side_effects=True, vmem_limit_bytes=56 << 20
        ),
    )(
        weight.T,
        features,
        band_tiles,
        tile_live.T,
        send_rows[0],
        recv_rows[0],
        edge_weight[0],
        live_slots,
        bias_terms.reshape(1, width),
        cotangent,
    )
    output, feature_grad, wg, bg = pl.pallas_call(
        finish,
        out_shape=tuple(jax.ShapeDtypeStruct(*r) for r in results),
        in_specs=[vmem] * 4,
        out_specs=(hbm,) * 4,
        scratch_shapes=[dma((4,))],
        compiler_params=pltpu.CompilerParams(vmem_limit_bytes=4 << 20),
    )(*parts)
    return (output, feature_grad, wg.T, bg.reshape(width))


def solution(mesh):
    return jax.shard_map(
        on_device,
        mesh=mesh,
        in_specs=(
            P(None, "dom"),
            P(None, "hid"),
            P(None, "dom"),
            P(None, "dom"),
            P("dom", None, None),
            P("dom", None, None),
            P("dom", None, None),
            P("dom", None),
            P("hid"),
            P("hid", "dom"),
        ),
        out_specs=(P("hid", "dom"), P("hid", "dom"), P(None, "hid"), P("hid")),
        check_vma=False,
    )
```

time: 81.9 us -> 76.4 us (0.933)
  the two profiles are of different devices: /device:TPU:1 before, /device:TPU:2 now
where the time goes in v2:
time: 76.4 us; the launch traced here: 76.3 us
  Pallas kernels  75.7 us (99%)
    pallas_call x1, Pallas kernels, on_device(): pl.pallas_call(kernel, out_shape=tuple((pltpu.VMEM(*r) for r in results))...  74.9 us

profile of v2, /device:TPU:2, one launch (start us, length us, event | category | flops | bytes accessed | tf_op | source)
XLA Modules:
  0.0 76.3 jit_solution(13035289609616471829)
XLA Ops:
  0.6 74.9 %shard_map.129 = (bf16[64,1024]{1,0:T(8,128)(2,1)S(1)}, bf16[64,1024]{1,0:T(8,128)(2,1)S(1)}, f32[64,512]{1,0:T(8,128)S(1)}, f32[1,64]{1,0:T(1,128)S(1)}) custom-call(bf16[64,512]{1,0:T(8,128)(2,1)} %bitcast.8, bf16[512,1024]{1,0:T(8,128)(2,1)} %feat_hbm.1, bf16[3072,1024]{1,0:T(8,128)(2,1)} %band_hbm.1, s32[4,12]{1,0:T(4,128)} %bitcast.12, ...), custom_call_target="tpu_custom_call" | custom-call | tf_op jit(solution)/shard_map/pallas_call | solution.py:506
  75.6 0.8 %shard_map.130 = (bf16[64,1024]{1,0:T(8,128)(2,1)}, bf16[64,1024]{1,0:T(8,128)(2,1)}, f32[64,512]{1,0:T(8,128)}, f32[1,64]{1,0:T(1,128)}) custom-call(bf16[64,1024]{1,0:T(8,128)(2,1)S(1)} %get-tuple-element.12.refs_0_, bf16[64,1024]{1,0:T(8,128)(2,1)S(1)} %get-tuple-element.13.refs_1_, f32[64,512]{1,0:T(8,128)S(1)} %get-tuple-element.14.refs_2_, ...), custom_call_target="tpu_custom_call" | custom-call | tf_op jit(solution)/shard_map/pallas_call | solution.py:580

commit v3 on v2

--- a/solution.py
+++ b/solution.py
@@ -11,7 +11,7 @@
 TILE = 256
 NT = (((1,), (1,)), ((), ()))
 ZS = 8
-CHIPS = 16
+LISTS = 4
 BLOCKS = 32
 HIDS = 8
 
@@ -57,12 +57,15 @@
     bias_ref,
     cot,
     mapped,
+    mapped_tiles,
     near,
     picks,
     puts,
     weights,
     acc,
+    sparse,
     pre,
+    pre_tiles,
     term,
     term_in,
     out1,
@@ -104,7 +107,6 @@
     core = lax.rem(me, 2)
     z = lax.rem(me // 2, ZS)
     yh = me // (2 * ZS)
-    own = yh * ZS + z
     left = lax.rem(me + BLOCKS - 1, BLOCKS)
     right = lax.rem(me + 1, BLOCKS)
     rows = mapped.shape[1]
@@ -137,15 +139,39 @@
             device_id=where, device_id_type=MESH,
         )
 
-    def place(k):
-        step = k // 2
+    def offset(step):
         far = (step + 1) // 2
-        dz = lax.rem(4 + far * (1 - 2 * lax.rem(step, 2)) + ZS, ZS)
-        dy = 1 - lax.rem(k, 2)
-        slot = 2 * dz + dy
-        back = 2 * lax.rem(ZS - dz, ZS) + dy
-        chip = lax.rem(yh + dy, 2) * ZS + lax.rem(z + dz, ZS)
-        return slot, back, chip
+        return lax.rem(4 + far * (1 - 2 * lax.rem(step, 2)) + ZS, ZS)
+
+    def chip_at(dz, dy):
+        return lax.rem(yh + dy, 2) * ZS + lax.rem(z + dz, ZS)
+
+    def list_row(ref, dz):
+        return jnp.concatenate(
+            [ref[pl.ds(2 * chip_at(dz, dy) + c, 1), :] for dy in range(2) for c in range(2)], axis=1
+        )
+
+    def onehot(index):
+        at = lax.broadcasted_iota(jnp.int32, (TILE, LISTS * 128), 0)
+        return jnp.where(at == index % TILE, 1.0, 0.0).astype(BF16)
+
+    def from_tiles(stacked, index):
+        tile = index // TILE
+        height = stacked.shape[0] // 4
+        got = stacked[3 * height:]
+        for t in range(3):
+            got = jnp.where(tile == t, stacked[t * height:(t + 1) * height], got)
+        return got
+
+    def to_tiles(values, index):
+        tile = index // TILE
+        return jnp.concatenate(
+            [jnp.where(tile == t, values, 0.0).astype(BF16) for t in range(4)], axis=0
+        )
+
+    def side_by_side(stacked):
+        height = stacked.shape[0] // 4
+        return jnp.concatenate([stacked[t * height:(t + 1) * height] for t in range(4)], axis=1)
 
     for load in loads[:4]:
         load.wait()
@@ -153,7 +179,9 @@
     @pl.loop(0, rows // TILE)
     def _(j):
         cols = pl.ds(pl.multiple_of(j * TILE, TILE), TILE)
-        mapped[:, cols] = dot(wt_ref[...], feat[:, cols]).astype(BF16)
+        got = dot(wt_ref[...], feat[:, cols]).astype(BF16)
+        mapped[:, cols] = got
+        mapped_tiles[pl.ds(pl.multiple_of(j * width, width), width), :] = got
 
     pl.semaphore_wait(barrier, BLOCKS - 1 + HIDS - 1)
 
@@ -162,55 +190,64 @@
     to_right.start()
     to_left.start()
 
-    def onehot(ref, chip):
-        index = jnp.concatenate(
-            [ref[pl.ds(2 * chip, 1), :], ref[pl.ds(2 * chip + 1, 1), :]], axis=1
+    def pick(dz):
+        index = list_row(send_ref, dz)
+        picks[dz] = onehot(index)
+        got = from_tiles(dot(mapped_tiles[...], picks[dz]), index).astype(BF16)
+        for h in range(2):
+            for i in range(LISTS):
+                out1[h, dz, i] = got[h * half:(h + 1) * half, i * 128:(i + 1) * 128]
+
+    def buffers(first):
+        return (out1, in1, a1_send, a1_recv) if first else (out2, in2, a2_send, a2_recv)
+
+    def ship(first, h, dz, dy, c):
+        outs, ins, ssem, rsem = buffers(first)
+        back = lax.rem(ZS - dz, ZS)
+        return remote(
+            outs.at[h, dz, 2 * dy + c], ins.at[h, back, 2 * dy + core],
+            ssem.at[h, dz, 2 * dy + c], rsem.at[h, back, 2 * dy + core],
+            dom=2 * chip_at(dz, dy) + c,
         )
-        at = lax.broadcasted_iota(jnp.int32, (rows, 2 * 128), 0)
-        return jnp.where(at == index, 1.0, 0.0).astype(BF16)
-
-    def slot_row(chip):
-        return jnp.concatenate(
-            [weights[pl.ds(2 * chip, 1), :], weights[pl.ds(2 * chip + 1, 1), :]], axis=1
-        )
-
-    def pick(slot, chip):
-        picks[slot] = onehot(send_ref, chip)
-        got = dot(mapped[...], picks[slot]).astype(BF16)
-        for h in range(2):
+
+    def ship_four(first, h, dz):
+        for dy in (1, 0):
             for c in range(2):
-                out1[h, slot, c] = got[h * half:(h + 1) * half, c * 128:(c + 1) * 128]
-
-    def ship(first, h, slot, back, chip, c):
-        outs, ins, ssem, rsem = (out1, in1, a1_send, a1_recv) if first else (out2, in2, a2_send, a2_recv)
-        return remote(
-            outs.at[h, slot, c], ins.at[h, back, core], ssem.at[h, slot, c], rsem.at[h, back, core],
-            dom=2 * chip + c,
-        )
-
-    def arrive(first, h, slot, c):
-        outs, ins, ssem, rsem = (out1, in1, a1_send, a1_recv) if first else (out2, in2, a2_send, a2_recv)
-        remote(
-            outs.at[h, slot, c], ins.at[h, slot, c], ssem.at[h, slot, c], rsem.at[h, slot, c], dom=left
-        ).wait_recv()
-
-    @pl.loop(0, CHIPS - 1)
-    def _(k):
-        slot, back, chip = place(k)
-        pick(slot, chip)
+                ship(first, h, dz, dy, c).start()
+
+    def ship_near(first, h):
+        outs, ins, _, _ = buffers(first)
         for c in range(2):
-            ship(True, 0, slot, back, chip, c).start()
-
-    pick(0, own)
-    for h in range(2):
-        ship(True, h, 0, 0, own, 1 - core).start()
-        in1[h, 0, core] = out1[h, 0, core]
-
-    @pl.loop(0, CHIPS - 1)
-    def _(k):
-        slot, back, chip = place(k)
-        for c in range(2):
-            ship(True, 1, slot, back, chip, c).start()
+            ship(first, h, 0, 1, c).start()
+        ship(first, h, 0, 0, 1 - core).start()
+        ins[h, 0, core] = outs[h, 0, core]
+
+    def arrive(first, h, dz, i):
+        outs, ins, ssem, rsem = buffers(first)
+        remote(outs.at[h, dz, i], ins.at[h, dz, i], ssem.at[h, dz, i], rsem.at[h, dz, i], dom=left).wait_recv()
+
+    def arrive_four(first, h, dz):
+        for i in (2, 3, 0, 1):
+            arrive(first, h, dz, i)
+
+    def arrive_near(first, h):
+        for i in (2, 3, 1 - core):
+            arrive(first, h, 0, i)
+
+    @pl.loop(0, ZS - 1)
+    def _(step):
+        dz = offset(step)
+        pick(dz)
+        ship_four(True, 0, dz)
+
+    pick(0)
+    ship_near(True, 0)
+
+    @pl.loop(0, ZS - 1)
+    def _(step):
+        ship_four(True, 1, offset(step))
+
+    ship_near(True, 1)
 
     for load in loads[4:]:
         load.wait()
@@ -247,10 +284,9 @@
 
     dense_forward(mapped, 1)
 
-    @pl.loop(0, CHIPS)
-    def _(k):
-        slot, _, chip = place(k)
-        puts[slot] = onehot(recv_ref, chip)
+    @pl.loop(0, ZS)
+    def _(dz):
+        puts[dz] = onehot(list_row(recv_ref, dz))
 
     to_right.wait_recv()
     dense_forward(near.at[0], 0)
@@ -259,43 +295,48 @@
 
     bias_in_col = row_to_column(bias_ref[...], width)
 
-    def put(h, slot, chip):
-        pair = jnp.concatenate([in1[h, slot, 0], in1[h, slot, 1]], axis=1).astype(F32)
-        acc[h * half:(h + 1) * half] += dot_nt((pair * slot_row(chip)).astype(BF16), puts[slot])
+    def lists_in(ins, h, dz):
+        return jnp.concatenate([ins[h, dz, i] for i in range(LISTS)], axis=1).astype(F32)
+
+    def put(h, dz):
+        values = lists_in(in1, h, dz) * list_row(weights, dz)
+        sparse[h] += dot_nt(to_tiles(values, list_row(recv_ref, dz)), puts[dz])
 
     def activate(h):
         part = slice(h * half, (h + 1) * half)
-        arrive(True, h, 0, 1 - core)
-        put(h, 0, own)
-
-        @pl.loop(0, CHIPS - 1)
-        def _(k):
-            slot, _, chip = place(k)
-            for c in range(2):
-                arrive(True, h, slot, c)
-            put(h, slot, chip)
-
-        act = acc[part] + bias_in_col[part]
+        sparse[h] = jnp.zeros_like(sparse[h])
+
+        @pl.loop(0, ZS - 1)
+        def _(step):
+            dz = offset(step)
+            arrive_four(True, h, dz)
+            put(h, dz)
+
+        arrive_near(True, h)
+        put(h, 0)
+        act = acc[part] + bias_in_col[part] + side_by_side(sparse[h])
         gate = 1.0 / (1.0 + jnp.exp(-act))
         out_ref[part] = (act * gate).astype(BF16)
-        pre[part] = (cot[part].astype(F32) * (gate * (1.0 + act * (1.0 - gate)))).astype(BF16)
-
-    def message(h, slot, chip):
-        got = (dot(pre[h * half:(h + 1) * half], puts[slot]) * slot_row(chip)).astype(BF16)
-        out2[h, slot, 0] = got[:, :128]
-        out2[h, slot, 1] = got[:, 128:]
+        grad = (cot[part].astype(F32) * (gate * (1.0 + act * (1.0 - gate)))).astype(BF16)
+        pre[part] = grad
+        for t in range(4):
+            pre_tiles[h, t * half:(t + 1) * half] = grad[:, t * TILE:(t + 1) * TILE]
+
+    def message(h, dz):
+        got = from_tiles(dot(pre_tiles[h], puts[dz]), list_row(recv_ref, dz))
+        got = (got * list_row(weights, dz)).astype(BF16)
+        for i in range(LISTS):
+            out2[h, dz, i] = got[:, i * 128:(i + 1) * 128]
 
     def send_messages(h):
-        @pl.loop(0, CHIPS - 1)
-        def _(k):
-            slot, back, chip = place(k)
-            message(h, slot, chip)
-            for c in range(2):
-                ship(False, h, slot, back, chip, c).start()
-
-        message(h, 0, own)
-        ship(False, h, 0, 0, own, 1 - core).start()
-        in2[h, 0, core] = out2[h, 0, core]
+        @pl.loop(0, ZS - 1)
+        def _(step):
+            dz = offset(step)
+            message(h, dz)
+            ship_four(False, h, dz)
+
+        message(h, 0)
+        ship_near(False, h)
 
     def dense_backward(target, s):
         @pl.loop(0, rows // TILE)
@@ -353,23 +394,22 @@
     grad_right.wait_recv()
     acc[...] += term_in[0].astype(F32) + term_in[1].astype(F32)
 
-    def give_back(h, slot):
-        pair = jnp.concatenate([in2[h, slot, 0], in2[h, slot, 1]], axis=1)
-        acc[h * half:(h + 1) * half] += dot_nt(pair, picks[slot])
+    def give_back(h, dz):
+        sparse[h] += dot_nt(to_tiles(lists_in(in2, h, dz), list_row(send_ref, dz)), picks[dz])
 
     def gradient(h):
-        arrive(False, h, 0, 1 - core)
+        part = slice(h * half, (h + 1) * half)
+        sparse[h] = jnp.zeros_like(sparse[h])
+
+        @pl.loop(0, ZS - 1)
+        def _(step):
+            dz = offset(step)
+            arrive_four(False, h, dz)
+            give_back(h, dz)
+
+        arrive_near(False, h)
         give_back(h, 0)
-
-        @pl.loop(0, CHIPS - 1)
-        def _(k):
-            slot, _, chip = place(k)
-            for c in range(2):
-                arrive(False, h, slot, c)
-            give_back(h, slot)
-
-        part = slice(h * half, (h + 1) * half)
-        gb[0, part] = acc[part].astype(BF16)
+        gb[0, part] = (acc[part] + side_by_side(sparse[h])).astype(BF16)
 
     def share(h, j):
         part = pl.ds(h * half, half)
@@ -445,17 +485,19 @@
     for step in range(5):
         bias_copy(step).wait_send()
 
-    @pl.loop(0, CHIPS - 1)
-    def _(k):
-        slot, back, chip = place(k)
+    @pl.loop(1, ZS)
+    def _(dz):
+        for first in (True, False):
+            for h in range(2):
+                for dy in range(2):
+                    for c in range(2):
+                        ship(first, h, dz, dy, c).wait_send()
+
+    for first in (True, False):
         for h in range(2):
             for c in range(2):
-                ship(True, h, slot, back, chip, c).wait_send()
-                ship(False, h, slot, back, chip, c).wait_send()
-
-    for h in range(2):
-        ship(True, h, 0, 0, own, 1 - core).wait_send()
-        ship(False, h, 0, 0, own, 1 - core).wait_send()
+                ship(first, h, 0, 1, c).wait_send()
+            ship(first, h, 0, 0, 1 - core).wait_send()
 
     @pl.loop(1, HIDS)
     def _(j):
@@ -501,7 +543,7 @@
     hbm = pl.BlockSpec(memory_space=pltpu.HBM)
     dma = pltpu.SemaphoreType.DMA
     block = pltpu.VMEM((width, rows), BF16)
-    lists = pltpu.VMEM((2, CHIPS, 2, width // 2, 128), BF16)
+    lists = pltpu.VMEM((2, ZS, LISTS, width // 2, 128), BF16)
     results = (((width, rows), BF16), ((width, rows), BF16), ((width, depth), F32), ((1, width), F32))
     parts = pl.pallas_call(
         kernel,
@@ -520,12 +562,15 @@
             pltpu.VMEM((1, width), F32),
             block,
             block,
+            pltpu.VMEM((4 * width, TILE), BF16),
             pltpu.VMEM((2, width, rows), BF16),
-            pltpu.VMEM((CHIPS, rows, 256), BF16),
-            pltpu.VMEM((CHIPS, rows, 256), BF16),
+            pltpu.VMEM((ZS, TILE, LISTS * 128), BF16),
+            pltpu.VMEM((ZS, TILE, LISTS * 128), BF16),
             pltpu.VMEM((BLOCKS, 128), F32),
             pltpu.VMEM((width, rows), F32),
+            pltpu.VMEM((2, 2 * width, TILE), F32),
             block,
+            pltpu.VMEM((2, 2 * width, TILE), BF16),
             pltpu.VMEM((2, width, rows), BF16),
             pltpu.VMEM((2, width, rows), BF16),
             lists,
@@ -543,12 +588,12 @@
             pltpu.VMEM((8, 128), F32),
             pltpu.VMEM((BLOCKS, 8, 128), F32),
             dma((10,)),
-            dma((2, CHIPS, 2)),
-            dma((2, CHIPS, 2)),
+            dma((2, ZS, LISTS)),
+            dma((2, ZS, LISTS)),
             dma((2,)),
             dma((2,)),
-            dma((2, CHIPS, 2)),
-            dma((2, CHIPS, 2)),
+            dma((2, ZS, LISTS)),
+            dma((2, ZS, LISTS)),
             dma((2,)),
             dma((2,)),
             dma((HIDS,)),

time: 76.4 us -> 67.6 us (0.88)
  the two profiles are of different devices: /device:TPU:2 before, /device:TPU:1 now
where the time goes in v3:
time: 67.6 us; the launch traced here: 66.9 us
  Pallas kernels  66.2 us (98%)
    pallas_call x1, Pallas kernels, on_device(): pl.pallas_call(kernel, out_shape=tuple((pltpu.VMEM(*r) for r in results))...  65.4 us

profile of v3, /device:TPU:1, one launch (start us, length us, event | category | flops | bytes accessed | tf_op | source)
XLA Modules:
  0.0 66.9 jit_solution(13893580759182121100)
XLA Ops:
  0.6 65.4 %shard_map.129 = (bf16[64,1024]{1,0:T(8,128)(2,1)S(1)}, bf16[64,1024]{1,0:T(8,128)(2,1)S(1)}, f32[64,512]{1,0:T(8,128)S(1)}, f32[1,64]{1,0:T(1,128)S(1)}) custom-call(bf16[64,512]{1,0:T(8,128)(2,1)} %bitcast.8, bf16[512,1024]{1,0:T(8,128)(2,1)} %feat_hbm.1, bf16[3072,1024]{1,0:T(8,128)(2,1)} %band_hbm.1, s32[4,12]{1,0:T(4,128)} %bitcast.12, ...), custom_call_target="tpu_custom_call" | custom-call | tf_op jit(solution)/shard_map/pallas_call | solution.py:548
  66.1 0.8 %shard_map.130 = (bf16[64,1024]{1,0:T(8,128)(2,1)}, bf16[64,1024]{1,0:T(8,128)(2,1)}, f32[64,512]{1,0:T(8,128)}, f32[1,64]{1,0:T(1,128)}) custom-call(bf16[64,1024]{1,0:T(8,128)(2,1)S(1)} %get-tuple-element.12.refs_0_, bf16[64,1024]{1,0:T(8,128)(2,1)S(1)} %get-tuple-element.13.refs_1_, f32[64,512]{1,0:T(8,128)S(1)} %get-tuple-element.14.refs_2_, ...), custom_call_target="tpu_custom_call" | custom-call | tf_op jit(solution)/shard_map/pallas_call | solution.py:625

commit v4 on v3

--- a/solution.py
+++ b/solution.py
@@ -196,7 +196,7 @@
         got = from_tiles(dot(mapped_tiles[...], picks[dz]), index).astype(BF16)
         for h in range(2):
             for i in range(LISTS):
-                out1[h, dz, i] = got[h * half:(h + 1) * half, i * 128:(i + 1) * 128]
+                out1[h, LISTS * dz + i] = got[h * half:(h + 1) * half, i * 128:(i + 1) * 128]
 
     def buffers(first):
         return (out1, in1, a1_send, a1_recv) if first else (out2, in2, a2_send, a2_recv)
@@ -205,10 +205,14 @@
         outs, ins, ssem, rsem = buffers(first)
         back = lax.rem(ZS - dz, ZS)
         return remote(
-            outs.at[h, dz, 2 * dy + c], ins.at[h, back, 2 * dy + core],
-            ssem.at[h, dz, 2 * dy + c], rsem.at[h, back, 2 * dy + core],
-            dom=2 * chip_at(dz, dy) + c,
+            outs.at[h, LISTS * dz + 2 * dy + c], ins.at[h, LISTS * back + 2 * dy + core],
+            ssem.at[h], rsem.at[h, back], dom=2 * chip_at(dz, dy) + c,
         )
+
+    def sent(first, h):
+        outs, ins, ssem, rsem = buffers(first)
+        every = pl.ds(1, BLOCKS - 1)
+        remote(outs.at[h, every], ins.at[h, every], ssem.at[h], rsem.at[h, 0], dom=left).wait_send()
 
     def ship_four(first, h, dz):
         for dy in (1, 0):
@@ -220,19 +224,18 @@
         for c in range(2):
             ship(first, h, 0, 1, c).start()
         ship(first, h, 0, 0, 1 - core).start()
-        ins[h, 0, core] = outs[h, 0, core]
-
-    def arrive(first, h, dz, i):
+        ins[h, core] = outs[h, core]
+
+    def arrive(first, h, dz, count):
         outs, ins, ssem, rsem = buffers(first)
-        remote(outs.at[h, dz, i], ins.at[h, dz, i], ssem.at[h, dz, i], rsem.at[h, dz, i], dom=left).wait_recv()
+        these = pl.ds(LISTS * dz, count)
+        remote(outs.at[h, these], ins.at[h, these], ssem.at[h], rsem.at[h, dz], dom=left).wait_recv()
 
     def arrive_four(first, h, dz):
-        for i in (2, 3, 0, 1):
-            arrive(first, h, dz, i)
+        arrive(first, h, dz, LISTS)
 
     def arrive_near(first, h):
-        for i in (2, 3, 1 - core):
-            arrive(first, h, 0, i)
+        arrive(first, h, 0, LISTS - 1)
 
     @pl.loop(0, ZS - 1)
     def _(step):
@@ -261,7 +264,7 @@
     @pl.loop(1, HIDS)
     def _(j):
         peer = lax.rem(hid + j, HIDS)
-        remote(wsend.at[peer], wrecv.at[HIDS - j], w_send.at[j], w_recv.at[HIDS - j], hid=peer).start()
+        remote(wsend.at[peer], wrecv.at[HIDS - j], w_send.at[0], w_recv.at[0], hid=peer).start()
 
     slot_ids = lax.broadcasted_iota(jnp.int32, (BLOCKS, 128), 1).astype(F32)
     counts = row_to_column(slots_ref[...].astype(F32), BLOCKS)
@@ -296,7 +299,7 @@
     bias_in_col = row_to_column(bias_ref[...], width)
 
     def lists_in(ins, h, dz):
-        return jnp.concatenate([ins[h, dz, i] for i in range(LISTS)], axis=1).astype(F32)
+        return jnp.concatenate([ins[h, LISTS * dz + i] for i in range(LISTS)], axis=1).astype(F32)
 
     def put(h, dz):
         values = lists_in(in1, h, dz) * list_row(weights, dz)
@@ -326,7 +329,7 @@
         got = from_tiles(dot(pre_tiles[h], puts[dz]), list_row(recv_ref, dz))
         got = (got * list_row(weights, dz)).astype(BF16)
         for i in range(LISTS):
-            out2[h, dz, i] = got[:, i * 128:(i + 1) * 128]
+            out2[h, LISTS * dz + i] = got[:, i * 128:(i + 1) * 128]
 
     def send_messages(h):
         @pl.loop(0, ZS - 1)
@@ -366,25 +369,26 @@
     send_messages(0)
     activate(1)
 
+    bias_col = jnp.sum(pre[...].astype(F32), axis=1, keepdims=True)
+    diagonal = lax.broadcasted_iota(jnp.int32, (width, 128), 0) == lax.broadcasted_iota(jnp.int32, (width, 128), 1)
+    bias_row = jnp.sum(jnp.where(diagonal, bias_col, 0.0), axis=0, keepdims=True)
+    bias_out[0] = jnp.broadcast_to(bias_row, (8, 128))
+    bias_copy(0).start()
     dense_backward(term.at[0], 0)
     grad_left = remote(term.at[0], term_in.at[0], n2_send.at[0], n2_recv.at[0], dom=left)
     grad_left.start()
     dense_backward(term.at[1], 2)
     grad_right = remote(term.at[1], term_in.at[1], n2_send.at[1], n2_recv.at[1], dom=right)
     grad_right.start()
-    bias_col = jnp.sum(pre[...].astype(F32), axis=1, keepdims=True)
-    diagonal = lax.broadcasted_iota(jnp.int32, (width, 128), 0) == lax.broadcasted_iota(jnp.int32, (width, 128), 1)
-    bias_row = jnp.sum(jnp.where(diagonal, bias_col, 0.0), axis=0, keepdims=True)
-    bias_out[0] = jnp.broadcast_to(bias_row, (8, 128))
-    bias_copy(0).start()
+    bias_step(0)
     send_messages(1)
-    bias_step(0)
 
     dense_backward(acc, 1)
 
-    @pl.loop(1, HIDS)
-    def _(j):
-        remote(wsend.at[j], wrecv.at[j], w_send.at[j], w_recv.at[j], dom=left).wait_recv()
+    peers = pl.ds(1, HIDS - 1)
+    slices = remote(wsend.at[peers], wrecv.at[peers], w_send.at[0], w_recv.at[0], dom=left)
+    slices.wait_recv()
+    slices.wait_send()
 
     wfull[...] = jnp.transpose(
         wrecv[...].reshape(HIDS * width, 128).astype(F32), (1, 0)
@@ -414,15 +418,20 @@
     def share(h, j):
         part = pl.ds(h * half, half)
         return remote(
-            gb.at[0, part], gb.at[HIDS - j, part], g_send.at[h, j], g_recv.at[h, HIDS - j],
+            gb.at[0, part], gb.at[HIDS - j, part], g_send.at[h], g_recv.at[h],
             hid=lax.rem(hid + j, HIDS),
         )
+
+    def shared(h):
+        part = pl.ds(h * half, half)
+        return remote(gb.at[peers, part], gb.at[peers, part], g_send.at[h], g_recv.at[h], dom=left)
 
     def share_all(h):
         @pl.loop(1, HIDS)
         def _(j):
             share(h, j).start()
 
+    bias_step(1)
     gradient(0)
     share_all(0)
     gradient(1)
@@ -430,36 +439,41 @@
     wg = dot_nt(gb[0], feat[...])
     for d in range(BLOCKS):
         r, c = d // 4, d % 4
-        pieces[d] = wg[8 * r:8 * r + 8, 128 * c:128 * c + 128]
+        pieces[d] = wg[8 * r:8 * r + 8, 128 * c:128 * c + 128].astype(BF16)
+
+    def reduce_piece(j):
+        peer = lax.rem(me + j, BLOCKS)
+        return remote(pieces.at[peer], pieces_in.at[BLOCKS - j], rs_send.at[0], rs_recv.at[0], dom=peer)
+
+    def spread_piece(j):
+        return remote(summed, wg_all.at[me], ag_send.at[0], ag_recv.at[0], dom=lax.rem(me + j, BLOCKS))
 
     @pl.loop(1, BLOCKS)
     def _(j):
-        peer = lax.rem(me + j, BLOCKS)
-        remote(pieces.at[peer], pieces_in.at[BLOCKS - j], rs_send.at[j], rs_recv.at[BLOCKS - j], dom=peer).start()
+        reduce_piece(j).start()
 
     share_all(1)
-    bias_step(1)
-    summed[...] = pieces[me]
+    bias_step(2)
+    for h in range(2):
+        sent(True, h)
+        sent(False, h)
+
+    pieces_in[0] = pieces[me]
+    others = pl.ds(1, BLOCKS - 1)
+    reduced = remote(pieces.at[others], pieces_in.at[others], rs_send.at[0], rs_recv.at[0], dom=left)
+    reduced.wait_recv()
+    summed[...] = jnp.sum(pieces_in[...].astype(F32), axis=0).astype(BF16)
 
     @pl.loop(1, BLOCKS)
     def _(j):
-        remote(pieces.at[j], pieces_in.at[j], rs_send.at[j], rs_recv.at[j], dom=left).wait_recv()
-        summed[...] += pieces_in[j]
-
-    @pl.loop(1, BLOCKS)
-    def _(j):
-        peer = lax.rem(me + j, BLOCKS)
-        remote(summed, wg_all.at[me], ag_send.at[j], ag_recv.at[BLOCKS - j], dom=peer).start()
+        spread_piece(j).start()
 
     wg_all[me] = summed[...]
-    bias_step(2)
     bias_step(3)
+    reduced.wait_send()
 
     for h in range(2):
-        @pl.loop(1, HIDS)
-        def _(j):
-            part = pl.ds(h * half, half)
-            remote(gb.at[0, part], gb.at[j, part], g_send.at[h, j], g_recv.at[h, j], dom=left).wait_recv()
+        shared(h).wait_recv()
 
     @pl.loop(0, rows // TILE)
     def _(j):
@@ -470,13 +484,12 @@
     bias_step(4)
     bg_ref[...] = bias_out[5, 0:1, :width]
 
-    @pl.loop(1, BLOCKS)
-    def _(j):
-        remote(summed, wg_all.at[lax.rem(me + j, BLOCKS)], ag_send.at[j], ag_recv.at[j], dom=left).wait_recv()
+    spread = remote(pieces.at[others], wg_all.at[others], ag_send.at[0], ag_recv.at[0], dom=left)
+    spread.wait_recv()
 
     for d in range(BLOCKS):
         r, c = d // 4, d % 4
-        wg_ref[8 * r:8 * r + 8, 128 * c:128 * c + 128] = wg_all[d]
+        wg_ref[8 * r:8 * r + 8, 128 * c:128 * c + 128] = wg_all[d].astype(F32)
 
     to_right.wait_send()
     to_left.wait_send()
@@ -485,32 +498,9 @@
     for step in range(5):
         bias_copy(step).wait_send()
 
-    @pl.loop(1, ZS)
-    def _(dz):
-        for first in (True, False):
-            for h in range(2):
-                for dy in range(2):
-                    for c in range(2):
-                        ship(first, h, dz, dy, c).wait_send()
-
-    for first in (True, False):
-        for h in range(2):
-            for c in range(2):
-                ship(first, h, 0, 1, c).wait_send()
-            ship(first, h, 0, 0, 1 - core).wait_send()
-
-    @pl.loop(1, HIDS)
-    def _(j):
-        peer = lax.rem(hid + j, HIDS)
-        remote(wsend.at[peer], wrecv.at[HIDS - j], w_send.at[j], w_recv.at[HIDS - j], hid=peer).wait_send()
-        for h in range(2):
-            share(h, j).wait_send()
-
-    @pl.loop(1, BLOCKS)
-    def _(j):
-        peer = lax.rem(me + j, BLOCKS)
-        remote(pieces.at[peer], pieces_in.at[BLOCKS - j], rs_send.at[j], rs_recv.at[BLOCKS - j], dom=peer).wait_send()
-        remote(summed, wg_all.at[me], ag_send.at[j], ag_recv.at[BLOCKS - j], dom=peer).wait_send()
+    for h in range(2):
+        shared(h).wait_send()
+    spread.wait_send()
 
 
 def finish(*refs):
@@ -543,7 +533,7 @@
     hbm = pl.BlockSpec(memory_space=pltpu.HBM)
     dma = pltpu.SemaphoreType.DMA
     block = pltpu.VMEM((width, rows), BF16)
-    lists = pltpu.VMEM((2, ZS, LISTS, width // 2, 128), BF16)
+    lists = pltpu.VMEM((2, BLOCKS, width // 2, 128), BF16)
     results = (((width, rows), BF16), ((width, rows), BF16), ((width, depth), F32), ((1, width), F32))
     parts = pl.pallas_call(
         kernel,
@@ -583,29 +573,29 @@
             pltpu.VMEM((HIDS, width, rows), BF16),
             pltpu.VMEM((6, 8, 128), F32),
             pltpu.VMEM((5, 8, 128), F32),
-            pltpu.VMEM((BLOCKS, 8, 128), F32),
-            pltpu.VMEM((BLOCKS, 8, 128), F32),
-            pltpu.VMEM((8, 128), F32),
-            pltpu.VMEM((BLOCKS, 8, 128), F32),
+            pltpu.VMEM((BLOCKS, 8, 128), BF16),
+            pltpu.VMEM((BLOCKS, 8, 128), BF16),
+            pltpu.VMEM((8, 128), BF16),
+            pltpu.VMEM((BLOCKS, 8, 128), BF16),
             dma((10,)),
-            dma((2, ZS, LISTS)),
-            dma((2, ZS, LISTS)),
-            dma((2,)),
-            dma((2,)),
-            dma((2, ZS, LISTS)),
-            dma((2, ZS, LISTS)),
-            dma((2,)),
-            dma((2,)),
-            dma((HIDS,)),
-            dma((HIDS,)),
+            dma((2,)),
+            dma((2, ZS)),
+            dma((2,)),
+            dma((2,)),
+            dma((2,)),
+            dma((2, ZS)),
+            dma((2,)),
+            dma((2,)),
+            dma((1,)),
+            dma((1,)),
             dma((5,)),
             dma((5,)),
-            dma((2, HIDS)),
-            dma((2, HIDS)),
-            dma((BLOCKS,)),
-            dma((BLOCKS,)),
-            dma((BLOCKS,)),
-            dma((BLOCKS,)),
+            dma((2,)),
+            dma((2,)),
+            dma((1,)),
+            dma((1,)),
+            dma((1,)),
+            dma((1,)),
         ],
         compiler_params=pltpu.CompilerParams(
             collective_id=0, has_side_effects=True, vmem_limit_bytes=56 << 20

time: 67.6 us -> 60.7 us (0.90)
  Pallas kernels: 66.2 us -> 59.9 us
    pallas_call x1, Pallas kernels: 65.4 us -> 59.1 us  [on_device(): pl.pallas_call(kernel, out_shape=tuple((pltpu.VMEM(*r) for r in results))...]
where the time goes in v4:
time: 60.7 us; the launch traced here: 60.6 us
  Pallas kernels  59.9 us (99%)
  between operations  0.64 us (1%)
    pallas_call x1, Pallas kernels, on_device(): pl.pallas_call(kernel, out_shape=tuple((pltpu.VMEM(*r) for r in results))...  59.1 us

profile of v4, /device:TPU:1, one launch (start us, length us, event | category | flops | bytes accessed | tf_op | source)
XLA Modules:
  0.0 60.6 jit_solution(3920580680288325017)
XLA Ops:
  0.6 59.1 %shard_map.129 = (bf16[64,1024]{1,0:T(8,128)(2,1)S(1)}, bf16[64,1024]{1,0:T(8,128)(2,1)S(1)}, f32[64,512]{1,0:T(8,128)S(1)}, f32[1,64]{1,0:T(1,128)S(1)}) custom-call(bf16[64,512]{1,0:T(8,128)(2,1)} %bitcast.8, bf16[512,1024]{1,0:T(8,128)(2,1)} %feat_hbm.1, bf16[3072,1024]{1,0:T(8,128)(2,1)} %band_hbm.1, s32[4,12]{1,0:T(4,128)} %bitcast.12, ...), custom_call_target="tpu_custom_call" | custom-call | tf_op jit(solution)/shard_map/pallas_call | solution.py:538
  59.8 0.8 %shard_map.130 = (bf16[64,1024]{1,0:T(8,128)(2,1)}, bf16[64,1024]{1,0:T(8,128)(2,1)}, f32[64,512]{1,0:T(8,128)}, f32[1,64]{1,0:T(1,128)}) custom-call(bf16[64,1024]{1,0:T(8,128)(2,1)S(1)} %get-tuple-element.12.refs_0_, bf16[64,1024]{1,0:T(8,128)(2,1)S(1)} %get-tuple-element.13.refs_1_, f32[64,512]{1,0:T(8,128)S(1)} %get-tuple-element.14.refs_2_, ...), custom_call_target="tpu_custom_call" | custom-call | tf_op jit(solution)/shard_map/pallas_call | solution.py:615

commit v5 on v4

--- a/solution.py
+++ b/solution.py
@@ -14,6 +14,7 @@
 LISTS = 4
 BLOCKS = 32
 HIDS = 8
+XS = 4
 
 
 def dot(a, b):
@@ -261,10 +262,14 @@
         wsend[p, :, :width] = wt[:, p * width:(p + 1) * width]
     wrecv[0] = wsend[hid]
 
-    @pl.loop(1, HIDS)
-    def _(j):
-        peer = lax.rem(hid + j, HIDS)
-        remote(wsend.at[peer], wrecv.at[HIDS - j], w_send.at[0], w_recv.at[0], hid=peer).start()
+    def hid_at(dl, dx):
+        return lax.rem(hid // XS + dl, 2) * XS + lax.rem(lax.rem(hid, XS) + dx, XS)
+
+    for dl in range(2):
+        for dx in range(XS):
+            if dl + dx:
+                peer = hid_at(dl, dx)
+                remote(wsend.at[peer], wrecv.at[XS * dl + (XS - dx) % XS], w_send.at[0], w_recv.at[0], hid=peer).start()
 
     slot_ids = lax.broadcasted_iota(jnp.int32, (BLOCKS, 128), 1).astype(F32)
     counts = row_to_column(slots_ref[...].astype(F32), BLOCKS)
@@ -341,18 +346,32 @@
         message(h, 0)
         ship_near(False, h)
 
-    def dense_backward(target, s):
+    def dense_backward(h, target, s):
+        part = slice(h * half, (h + 1) * half)
+
         @pl.loop(0, rows // TILE)
         def _(t):
             cols = pl.ds(pl.multiple_of(t * TILE, TILE), TILE)
             parts = [
-                (pre[:, j * TILE:(j + 1) * TILE].astype(F32)
+                (pre[part, j * TILE:(j + 1) * TILE].astype(F32)
                  * live_ref[j, s * 4 + t].astype(F32)).astype(BF16)
                 for j in range(rows // TILE)
             ]
             band_rows = pl.ds(pl.multiple_of(s * rows + t * TILE, TILE), TILE)
             got = dot_nt(jnp.concatenate(parts, axis=1), band[band_rows, :])
-            target[:, cols] = got.astype(target.dtype)
+            target[part, cols] = got.astype(target.dtype)
+
+    def grad_move(h, side):
+        part = pl.ds(h * half, half)
+        return remote(
+            term.at[side, part], term_in.at[side, part], n2_send.at[h, side], n2_recv.at[h, side],
+            dom=(left, right)[side],
+        )
+
+    def dense_gradients(h):
+        for side in range(2):
+            dense_backward(h, term.at[side], 2 * side)
+            grad_move(h, side).start()
 
     def bias_copy(step):
         bit = 1 << step
@@ -367,23 +386,18 @@
 
     activate(0)
     send_messages(0)
+    dense_gradients(0)
+    dense_backward(0, acc, 1)
     activate(1)
-
+    send_messages(1)
     bias_col = jnp.sum(pre[...].astype(F32), axis=1, keepdims=True)
     diagonal = lax.broadcasted_iota(jnp.int32, (width, 128), 0) == lax.broadcasted_iota(jnp.int32, (width, 128), 1)
     bias_row = jnp.sum(jnp.where(diagonal, bias_col, 0.0), axis=0, keepdims=True)
     bias_out[0] = jnp.broadcast_to(bias_row, (8, 128))
     bias_copy(0).start()
-    dense_backward(term.at[0], 0)
-    grad_left = remote(term.at[0], term_in.at[0], n2_send.at[0], n2_recv.at[0], dom=left)
-    grad_left.start()
-    dense_backward(term.at[1], 2)
-    grad_right = remote(term.at[1], term_in.at[1], n2_send.at[1], n2_recv.at[1], dom=right)
-    grad_right.start()
+    dense_gradients(1)
     bias_step(0)
-    send_messages(1)
-
-    dense_backward(acc, 1)
+    dense_backward(1, acc, 1)
 
     peers = pl.ds(1, HIDS - 1)
     slices = remote(wsend.at[peers], wrecv.at[peers], w_send.at[0], w_recv.at[0], dom=left)
@@ -393,10 +407,6 @@
     wfull[...] = jnp.transpose(
         wrecv[...].reshape(HIDS * width, 128).astype(F32), (1, 0)
     )[:width].astype(BF16)
-
-    grad_left.wait_recv()
-    grad_right.wait_recv()
-    acc[...] += term_in[0].astype(F32) + term_in[1].astype(F32)
 
     def give_back(h, dz):
         sparse[h] += dot_nt(to_tiles(lists_in(in2, h, dz), list_row(send_ref, dz)), picks[dz])
@@ -413,27 +423,32 @@
 
         arrive_near(False, h)
         give_back(h, 0)
-        gb[0, part] = (acc[part] + side_by_side(sparse[h])).astype(BF16)
-
-    def share(h, j):
+        for side in range(2):
+            grad_move(h, side).wait_recv()
+        dense = acc[part] + (term_in[0, part].astype(F32) + term_in[1, part].astype(F32))
+        gb[0, part] = (dense + side_by_side(sparse[h])).astype(BF16)
+
+    def move(h, kind, src, dst, **where):
         part = pl.ds(h * half, half)
-        return remote(
-            gb.at[0, part], gb.at[HIDS - j, part], g_send.at[h], g_recv.at[h],
-            hid=lax.rem(hid + j, HIDS),
-        )
-
-    def shared(h):
-        part = pl.ds(h * half, half)
-        return remote(gb.at[peers, part], gb.at[peers, part], g_send.at[h], g_recv.at[h], dom=left)
-
-    def share_all(h):
-        @pl.loop(1, HIDS)
-        def _(j):
-            share(h, j).start()
-
-    bias_step(1)
+        return remote(gb.at[src, part], gb.at[dst, part], g_send.at[h, kind], g_recv.at[h, kind], **where)
+
+    def share(h):
+        move(h, 0, 0, XS, hid=hid_at(1, 0)).start()
+        for dx in (2, 1, 3):
+            move(h, 1, 0, XS - dx, hid=hid_at(0, dx)).start()
+
+    def forward(h):
+        move(h, 0, 0, XS, dom=left).wait_recv()
+        for dx in (2, 1, 3):
+            move(h, 2, XS, 2 * XS - dx, hid=hid_at(0, dx)).start()
+
+    def shared(h, kind):
+        these = pl.ds(1 if kind == 1 else XS + 1, XS - 1)
+        return move(h, kind, these, these, dom=left)
+
     gradient(0)
-    share_all(0)
+    share(0)
+    forward(0)
     gradient(1)
 
     wg = dot_nt(gb[0], feat[...])
@@ -452,7 +467,9 @@
     def _(j):
         reduce_piece(j).start()
 
-    share_all(1)
+    share(1)
+    bias_step(1)
+    forward(1)
     bias_step(2)
     for h in range(2):
         sent(True, h)
@@ -473,7 +490,8 @@
     reduced.wait_send()
 
     for h in range(2):
-        shared(h).wait_recv()
+        for kind in (1, 2):
+            shared(h, kind).wait_recv()
 
     @pl.loop(0, rows // TILE)
     def _(j):
@@ -493,13 +511,14 @@
 
     to_right.wait_send()
     to_left.wait_send()
-    grad_left.wait_send()
-    grad_right.wait_send()
     for step in range(5):
         bias_copy(step).wait_send()
 
     for h in range(2):
-        shared(h).wait_send()
+        move(h, 0, 0, XS, dom=left).wait_send()
+        for side in range(2):
+            grad_move(h, side).wait_send()
+            shared(h, side + 1).wait_send()
     spread.wait_send()
 
 
@@ -584,14 +603,14 @@
             dma((2,)),
             dma((2,)),
             dma((2, ZS)),
-            dma((2,)),
-            dma((2,)),
+            dma((2, 2)),
+            dma((2, 2)),
             dma((1,)),
             dma((1,)),
             dma((5,)),
             dma((5,)),
-            dma((2,)),
-            dma((2,)),
+            dma((2, 3)),
+            dma((2, 3)),
             dma((1,)),
             dma((1,)),
             dma((1,)),

time: 60.7 us -> 59.5 us (0.980)
  Pallas kernels: 59.9 us -> 58.7 us
    pallas_call x1, Pallas kernels: 59.1 us -> 58 us  [on_device(): pl.pallas_call(kernel, out_shape=tuple((pltpu.VMEM(*r) for r in results))...]
where the time goes in v5:
time: 59.5 us; the launch traced here: 59.4 us
  Pallas kernels  58.7 us (99%)
  between operations  0.64 us (1%)
    pallas_call x1, Pallas kernels, on_device(): pl.pallas_call(kernel, out_shape=tuple((pltpu.VMEM(*r) for r in results))...  58 us

profile of v5, /device:TPU:1, one launch (start us, length us, event | category | flops | bytes accessed | tf_op | source)
XLA Modules:
  0.0 59.4 jit_solution(4400239004908666464)
XLA Ops:
  0.6 58.0 %shard_map.129 = (bf16[64,1024]{1,0:T(8,128)(2,1)S(1)}, bf16[64,1024]{1,0:T(8,128)(2,1)S(1)}, f32[64,512]{1,0:T(8,128)S(1)}, f32[1,64]{1,0:T(1,128)S(1)}) custom-call(bf16[64,512]{1,0:T(8,128)(2,1)} %bitcast.8, bf16[512,1024]{1,0:T(8,128)(2,1)} %feat_hbm.1, bf16[3072,1024]{1,0:T(8,128)(2,1)} %band_hbm.1, s32[4,12]{1,0:T(4,128)} %bitcast.12, ...), custom_call_target="tpu_custom_call" | custom-call | tf_op jit(solution)/shard_map/pallas_call | solution.py:557
  58.6 0.8 %shard_map.130 = (bf16[64,1024]{1,0:T(8,128)(2,1)}, bf16[64,1024]{1,0:T(8,128)(2,1)}, f32[64,512]{1,0:T(8,128)}, f32[1,64]{1,0:T(1,128)}) custom-call(bf16[64,1024]{1,0:T(8,128)(2,1)S(1)} %get-tuple-element.12.refs_0_, bf16[64,1024]{1,0:T(8,128)(2,1)S(1)} %get-tuple-element.13.refs_1_, f32[64,512]{1,0:T(8,128)S(1)} %get-tuple-element.14.refs_2_, ...), custom_call_target="tpu_custom_call" | custom-call | tf_op jit(solution)/shard_map/pallas_call | solution.py:634

commit v6 on v5

--- a/solution.py
+++ b/solution.py
@@ -12,9 +12,12 @@
 NT = (((1,), (1,)), ((), ()))
 ZS = 8
 LISTS = 4
+PARTS = ((0, 32), (32, 32))
 BLOCKS = 32
 HIDS = 8
 XS = 4
+ARRIVALS = ((4, 3, 5), (2, 6, 1), (7, 0))
+DEPARTURES = ((4, 3), (5, 2), (6, 1), (7,))
 
 
 def dot(a, b):
@@ -64,7 +67,6 @@
     puts,
     weights,
     acc,
-    sparse,
     pre,
     pre_tiles,
     term,
@@ -195,63 +197,58 @@
         index = list_row(send_ref, dz)
         picks[dz] = onehot(index)
         got = from_tiles(dot(mapped_tiles[...], picks[dz]), index).astype(BF16)
-        for h in range(2):
-            for i in range(LISTS):
-                out1[h, LISTS * dz + i] = got[h * half:(h + 1) * half, i * 128:(i + 1) * 128]
+        for i in range(LISTS):
+            out1[LISTS * dz + i] = got[:, i * 128:(i + 1) * 128]
 
     def buffers(first):
         return (out1, in1, a1_send, a1_recv) if first else (out2, in2, a2_send, a2_recv)
 
-    def ship(first, h, dz, dy, c):
+    def ship(first, p, dz, dy, c):
         outs, ins, ssem, rsem = buffers(first)
         back = lax.rem(ZS - dz, ZS)
+        part = pl.ds(*PARTS[p])
         return remote(
-            outs.at[h, LISTS * dz + 2 * dy + c], ins.at[h, LISTS * back + 2 * dy + core],
-            ssem.at[h], rsem.at[h, back], dom=2 * chip_at(dz, dy) + c,
+            outs.at[LISTS * dz + 2 * dy + c, part], ins.at[LISTS * back + 2 * dy + core, part],
+            ssem.at[p], rsem.at[p, back], dom=2 * chip_at(dz, dy) + c,
         )
 
-    def sent(first, h):
+    def sent(first, p):
         outs, ins, ssem, rsem = buffers(first)
-        every = pl.ds(1, BLOCKS - 1)
-        remote(outs.at[h, every], ins.at[h, every], ssem.at[h], rsem.at[h, 0], dom=left).wait_send()
-
-    def ship_four(first, h, dz):
+        every, part = pl.ds(1, BLOCKS - 1), pl.ds(*PARTS[p])
+        remote(outs.at[every, part], ins.at[every, part], ssem.at[p], rsem.at[p, 0], dom=left).wait_send()
+
+    def ship_four(first, p, dz):
         for dy in (1, 0):
             for c in range(2):
-                ship(first, h, dz, dy, c).start()
-
-    def ship_near(first, h):
+                ship(first, p, dz, dy, c).start()
+
+    def ship_near(first, p):
         outs, ins, _, _ = buffers(first)
+        part = pl.ds(*PARTS[p])
         for c in range(2):
-            ship(first, h, 0, 1, c).start()
-        ship(first, h, 0, 0, 1 - core).start()
-        ins[h, core] = outs[h, core]
-
-    def arrive(first, h, dz, count):
+            ship(first, p, 0, 1, c).start()
+        ship(first, p, 0, 0, 1 - core).start()
+        ins[core, part] = outs[core, part]
+
+    def arrive(first, p, dz, count):
         outs, ins, ssem, rsem = buffers(first)
-        these = pl.ds(LISTS * dz, count)
-        remote(outs.at[h, these], ins.at[h, these], ssem.at[h], rsem.at[h, dz], dom=left).wait_recv()
-
-    def arrive_four(first, h, dz):
-        arrive(first, h, dz, LISTS)
-
-    def arrive_near(first, h):
-        arrive(first, h, 0, LISTS - 1)
-
-    @pl.loop(0, ZS - 1)
-    def _(step):
-        dz = offset(step)
-        pick(dz)
-        ship_four(True, 0, dz)
+        these, part = pl.ds(LISTS * dz, count), pl.ds(*PARTS[p])
+        remote(outs.at[these, part], ins.at[these, part], ssem.at[p], rsem.at[p, dz], dom=left).wait_recv()
+
+    for batch in DEPARTURES:
+        for dz in batch:
+            pick(dz)
+        for dz in batch:
+            ship_four(True, 0, dz)
 
     pick(0)
     ship_near(True, 0)
-
-    @pl.loop(0, ZS - 1)
-    def _(step):
-        ship_four(True, 1, offset(step))
-
-    ship_near(True, 1)
+    for p in range(1, len(PARTS)):
+        @pl.loop(0, ZS - 1)
+        def _(step):
+            ship_four(True, p, offset(step))
+
+        ship_near(True, p)
 
     for load in loads[4:]:
         load.wait()
@@ -303,48 +300,53 @@
 
     bias_in_col = row_to_column(bias_ref[...], width)
 
-    def lists_in(ins, h, dz):
-        return jnp.concatenate([ins[h, LISTS * dz + i] for i in range(LISTS)], axis=1).astype(F32)
-
-    def put(h, dz):
-        values = lists_in(in1, h, dz) * list_row(weights, dz)
-        sparse[h] += dot_nt(to_tiles(values, list_row(recv_ref, dz)), puts[dz])
-
-    def activate(h):
-        part = slice(h * half, (h + 1) * half)
-        sparse[h] = jnp.zeros_like(sparse[h])
-
-        @pl.loop(0, ZS - 1)
-        def _(step):
-            dz = offset(step)
-            arrive_four(True, h, dz)
-            put(h, dz)
-
-        arrive_near(True, h)
-        put(h, 0)
-        act = acc[part] + bias_in_col[part] + side_by_side(sparse[h])
+    def lists_in(ins, p, dz):
+        part = pl.ds(*PARTS[p])
+        return jnp.concatenate([ins[LISTS * dz + i, part] for i in range(LISTS)], axis=1).astype(F32)
+
+    def stacked(p):
+        return slice(4 * PARTS[p][0], 4 * (PARTS[p][0] + PARTS[p][1]))
+
+    def collect(first, p, part_of):
+        total = None
+        for batch in ARRIVALS:
+            for dz in batch:
+                arrive(first, p, dz, LISTS if dz else LISTS - 1)
+            for dz in batch:
+                got = part_of(p, dz)
+                total = got if total is None else total + got
+        return side_by_side(total)
+
+    def put(p, dz):
+        values = lists_in(in1, p, dz) * list_row(weights, dz)
+        return dot_nt(to_tiles(values, list_row(recv_ref, dz)), puts[dz])
+
+    def activate(p):
+        start, size = PARTS[p]
+        part = slice(start, start + size)
+        act = collect(True, p, put) + acc[part] + bias_in_col[part]
         gate = 1.0 / (1.0 + jnp.exp(-act))
         out_ref[part] = (act * gate).astype(BF16)
         grad = (cot[part].astype(F32) * (gate * (1.0 + act * (1.0 - gate)))).astype(BF16)
         pre[part] = grad
         for t in range(4):
-            pre_tiles[h, t * half:(t + 1) * half] = grad[:, t * TILE:(t + 1) * TILE]
-
-    def message(h, dz):
-        got = from_tiles(dot(pre_tiles[h], puts[dz]), list_row(recv_ref, dz))
+            pre_tiles[4 * start + t * size:4 * start + (t + 1) * size] = grad[:, t * TILE:(t + 1) * TILE]
+
+    def message(p, dz):
+        got = from_tiles(dot(pre_tiles[stacked(p)], puts[dz]), list_row(recv_ref, dz))
         got = (got * list_row(weights, dz)).astype(BF16)
         for i in range(LISTS):
-            out2[h, LISTS * dz + i] = got[:, i * 128:(i + 1) * 128]
-
-    def send_messages(h):
-        @pl.loop(0, ZS - 1)
-        def _(step):
-            dz = offset(step)
-            message(h, dz)
-            ship_four(False, h, dz)
-
-        message(h, 0)
-        ship_near(False, h)
+            out2[LISTS * dz + i, pl.ds(*PARTS[p])] = got[:, i * 128:(i + 1) * 128]
+
+    def send_messages(p):
+        for batch in DEPARTURES:
+            for dz in batch:
+                message(p, dz)
+            for dz in batch:
+                ship_four(False, p, dz)
+
+        message(p, 0)
+        ship_near(False, p)
 
     def dense_backward(h, target, s):
         part = slice(h * half, (h + 1) * half)
@@ -384,12 +386,13 @@
         if step < 4:
             bias_copy(step + 1).start()
 
-    activate(0)
-    send_messages(0)
-    dense_gradients(0)
-    dense_backward(0, acc, 1)
-    activate(1)
-    send_messages(1)
+    for p, (start, size) in enumerate(PARTS):
+        activate(p)
+        send_messages(p)
+        if start + size == half:
+            dense_gradients(0)
+            dense_backward(0, acc, 1)
+
     bias_col = jnp.sum(pre[...].astype(F32), axis=1, keepdims=True)
     diagonal = lax.broadcasted_iota(jnp.int32, (width, 128), 0) == lax.broadcasted_iota(jnp.int32, (width, 128), 1)
     bias_row = jnp.sum(jnp.where(diagonal, bias_col, 0.0), axis=0, keepdims=True)
@@ -408,25 +411,18 @@
         wrecv[...].reshape(HIDS * width, 128).astype(F32), (1, 0)
     )[:width].astype(BF16)
 
-    def give_back(h, dz):
-        sparse[h] += dot_nt(to_tiles(lists_in(in2, h, dz), list_row(send_ref, dz)), picks[dz])
-
-    def gradient(h):
-        part = slice(h * half, (h + 1) * half)
-        sparse[h] = jnp.zeros_like(sparse[h])
-
-        @pl.loop(0, ZS - 1)
-        def _(step):
-            dz = offset(step)
-            arrive_four(False, h, dz)
-            give_back(h, dz)
-
-        arrive_near(False, h)
-        give_back(h, 0)
-        for side in range(2):
-            grad_move(h, side).wait_recv()
+    def give_back(p, dz):
+        return dot_nt(to_tiles(lists_in(in2, p, dz), list_row(send_ref, dz)), picks[dz])
+
+    def gradient(p):
+        start, size = PARTS[p]
+        part = slice(start, start + size)
+        returned = collect(False, p, give_back)
+        if start % half == 0:
+            for side in range(2):
+                grad_move(start // half, side).wait_recv()
         dense = acc[part] + (term_in[0, part].astype(F32) + term_in[1, part].astype(F32))
-        gb[0, part] = (dense + side_by_side(sparse[h])).astype(BF16)
+        gb[0, part] = (dense + returned).astype(BF16)
 
     def move(h, kind, src, dst, **where):
         part = pl.ds(h * half, half)
@@ -446,10 +442,11 @@
         these = pl.ds(1 if kind == 1 else XS + 1, XS - 1)
         return move(h, kind, these, these, dom=left)
 
-    gradient(0)
-    share(0)
-    forward(0)
-    gradient(1)
+    for p, (start, size) in enumerate(PARTS):
+        gradient(p)
+        if start + size == half:
+            share(0)
+            forward(0)
 
     wg = dot_nt(gb[0], feat[...])
     for d in range(BLOCKS):
@@ -471,9 +468,9 @@
     bias_step(1)
     forward(1)
     bias_step(2)
-    for h in range(2):
-        sent(True, h)
-        sent(False, h)
+    for p in range(len(PARTS)):
+        sent(True, p)
+        sent(False, p)
 
     pieces_in[0] = pieces[me]
     others = pl.ds(1, BLOCKS - 1)
@@ -552,7 +549,7 @@
     hbm = pl.BlockSpec(memory_space=pltpu.HBM)
     dma = pltpu.SemaphoreType.DMA
     block = pltpu.VMEM((width, rows), BF16)
-    lists = pltpu.VMEM((2, BLOCKS, width // 2, 128), BF16)
+    lists = pltpu.VMEM((BLOCKS, width, 128), BF16)
     results = (((width, rows), BF16), ((width, rows), BF16), ((width, depth), F32), ((1, width), F32))
     parts = pl.pallas_call(
         kernel,
@@ -577,9 +574,8 @@
             pltpu.VMEM((ZS, TILE, LISTS * 128), BF16),
             pltpu.VMEM((BLOCKS, 128), F32),
             pltpu.VMEM((width, rows), F32),
-            pltpu.VMEM((2, 2 * width, TILE), F32),
             block,
-            pltpu.VMEM((2, 2 * width, TILE), BF16),
+            pltpu.VMEM((4 * width, TILE), BF16),
             pltpu.VMEM((2, width, rows), BF16),
             pltpu.VMEM((2, width, rows), BF16),
             lists,
@@ -597,12 +593,12 @@
             pltpu.VMEM((8, 128), BF16),
             pltpu.VMEM((BLOCKS, 8, 128), BF16),
             dma((10,)),
-            dma((2,)),
-            dma((2, ZS)),
+            dma((len(PARTS),)),
+            dma((len(PARTS), ZS)),
             dma((2,)),
             dma((2,)),
-            dma((2,)),
-            dma((2, ZS)),
+            dma((len(PARTS),)),
+            dma((len(PARTS), ZS)),
             dma((2, 2)),
             dma((2, 2)),
             dma((1,)),

time: 59.5 us -> 57.6 us (0.968)
  Pallas kernels: 58.7 us -> 56.9 us
    pallas_call x1, Pallas kernels: 58 us -> 56.1 us  [on_device(): pl.pallas_call(kernel, out_shape=tuple((pltpu.VMEM(*r) for r in results))...]
where the time goes in v6:
time: 57.6 us; the launch traced here: 57.5 us
  Pallas kernels  56.9 us (99%)
  between operations  0.64 us (1%)
    pallas_call x1, Pallas kernels, on_device(): pl.pallas_call(kernel, out_shape=tuple((pltpu.VMEM(*r) for r in results))...  56.1 us

profile of v6, /device:TPU:1, one launch (start us, length us, event | category | flops | bytes accessed | tf_op | source)
XLA Modules:
  0.0 57.5 jit_solution(3795935113799524433)
XLA Ops:
  0.6 56.1 %shard_map.129 = (bf16[64,1024]{1,0:T(8,128)(2,1)S(1)}, bf16[64,1024]{1,0:T(8,128)(2,1)S(1)}, f32[64,512]{1,0:T(8,128)S(1)}, f32[1,64]{1,0:T(1,128)S(1)}) custom-call(bf16[64,512]{1,0:T(8,128)(2,1)} %bitcast.8, bf16[512,1024]{1,0:T(8,128)(2,1)} %feat_hbm.1, bf16[3072,1024]{1,0:T(8,128)(2,1)} %band_hbm.1, s32[4,12]{1,0:T(4,128)} %bitcast.12, ...), custom_call_target="tpu_custom_call" | custom-call | tf_op jit(solution)/shard_map/pallas_call | solution.py:554
  56.7 0.8 %shard_map.130 = (bf16[64,1024]{1,0:T(8,128)(2,1)}, bf16[64,1024]{1,0:T(8,128)(2,1)}, f32[64,512]{1,0:T(8,128)}, f32[1,64]{1,0:T(1,128)}) custom-call(bf16[64,1024]{1,0:T(8,128)(2,1)S(1)} %get-tuple-element.12.refs_0_, bf16[64,1024]{1,0:T(8,128)(2,1)S(1)} %get-tuple-element.13.refs_1_, f32[64,512]{1,0:T(8,128)S(1)} %get-tuple-element.14.refs_2_, ...), custom_call_target="tpu_custom_call" | custom-call | tf_op jit(solution)/shard_map/pallas_call | solution.py:630

commit v7 on v6

--- a/solution.py
+++ b/solution.py
@@ -307,9 +307,11 @@
     def stacked(p):
         return slice(4 * PARTS[p][0], 4 * (PARTS[p][0] + PARTS[p][1]))
 
-    def collect(first, p, part_of):
+    def collect(first, p, part_of, then=None):
         total = None
         for batch in ARRIVALS:
+            if then is not None and batch is ARRIVALS[1]:
+                then()
             for dz in batch:
                 arrive(first, p, dz, LISTS if dz else LISTS - 1)
             for dz in batch:
@@ -414,10 +416,10 @@
     def give_back(p, dz):
         return dot_nt(to_tiles(lists_in(in2, p, dz), list_row(send_ref, dz)), picks[dz])
 
-    def gradient(p):
+    def gradient(p, then=None):
         start, size = PARTS[p]
         part = slice(start, start + size)
-        returned = collect(False, p, give_back)
+        returned = collect(False, p, give_back, then)
         if start % half == 0:
             for side in range(2):
                 grad_move(start // half, side).wait_recv()
@@ -443,10 +445,9 @@
         return move(h, kind, these, these, dom=left)
 
     for p, (start, size) in enumerate(PARTS):
-        gradient(p)
+        gradient(p, (lambda: forward(0)) if start == half else None)
         if start + size == half:
             share(0)
-            forward(0)
 
     wg = dot_nt(gb[0], feat[...])
     for d in range(BLOCKS):

time: 57.6 us -> 57.1 us (level)
  no operation moved by 1% of the time
where the time goes in v7:
time: 57.1 us; the launch traced here: 57 us
  Pallas kernels  56.4 us (99%)
  between operations  0.64 us (1%)
    pallas_call x1, Pallas kernels, on_device(): pl.pallas_call(kernel, out_shape=tuple((pltpu.VMEM(*r) for r in results))...  55.6 us

profile of v7, /device:TPU:1, one launch (start us, length us, event | category | flops | bytes accessed | tf_op | source)
XLA Modules:
  0.0 57.0 jit_solution(8942728327633171499)
XLA Ops:
  0.6 55.6 %shard_map.129 = (bf16[64,1024]{1,0:T(8,128)(2,1)S(1)}, bf16[64,1024]{1,0:T(8,128)(2,1)S(1)}, f32[64,512]{1,0:T(8,128)S(1)}, f32[1,64]{1,0:T(1,128)S(1)}) custom-call(bf16[64,512]{1,0:T(8,128)(2,1)} %bitcast.8, bf16[512,1024]{1,0:T(8,128)(2,1)} %feat_hbm.1, bf16[3072,1024]{1,0:T(8,128)(2,1)} %band_hbm.1, s32[4,12]{1,0:T(4,128)} %bitcast.12, ...), custom_call_target="tpu_custom_call" | custom-call | tf_op jit(solution)/shard_map/pallas_call | solution.py:555
  56.3 0.8 %shard_map.130 = (bf16[64,1024]{1,0:T(8,128)(2,1)}, bf16[64,1024]{1,0:T(8,128)(2,1)}, f32[64,512]{1,0:T(8,128)}, f32[1,64]{1,0:T(1,128)}) custom-call(bf16[64,1024]{1,0:T(8,128)(2,1)S(1)} %get-tuple-element.12.refs_0_, bf16[64,1024]{1,0:T(8,128)(2,1)S(1)} %get-tuple-element.13.refs_1_, f32[64,512]{1,0:T(8,128)S(1)} %get-tuple-element.14.refs_2_, ...), custom_call_target="tpu_custom_call" | custom-call | tf_op jit(solution)/shard_map/pallas_call | solution.py:631

commit v8 on v7

--- a/solution.py
+++ b/solution.py
@@ -176,7 +176,7 @@
         height = stacked.shape[0] // 4
         return jnp.concatenate([stacked[t * height:(t + 1) * height] for t in range(4)], axis=1)
 
-    for load in loads[:4]:
+    for load in loads[:6]:
         load.wait()
 
     @pl.loop(0, rows // TILE)
@@ -185,13 +185,6 @@
         got = dot(wt_ref[...], feat[:, cols]).astype(BF16)
         mapped[:, cols] = got
         mapped_tiles[pl.ds(pl.multiple_of(j * width, width), width), :] = got
-
-    pl.semaphore_wait(barrier, BLOCKS - 1 + HIDS - 1)
-
-    to_right = remote(mapped, near.at[0], n1_send.at[0], n1_recv.at[0], dom=right)
-    to_left = remote(mapped, near.at[1], n1_send.at[1], n1_recv.at[1], dom=left)
-    to_right.start()
-    to_left.start()
 
     def pick(dz):
         index = list_row(send_ref, dz)
@@ -235,23 +228,16 @@
         these, part = pl.ds(LISTS * dz, count), pl.ds(*PARTS[p])
         remote(outs.at[these, part], ins.at[these, part], ssem.at[p], rsem.at[p, dz], dom=left).wait_recv()
 
-    for batch in DEPARTURES:
-        for dz in batch:
-            pick(dz)
-        for dz in batch:
-            ship_four(True, 0, dz)
-
-    pick(0)
-    ship_near(True, 0)
-    for p in range(1, len(PARTS)):
-        @pl.loop(0, ZS - 1)
-        def _(step):
-            ship_four(True, p, offset(step))
-
-        ship_near(True, p)
-
-    for load in loads[4:]:
-        load.wait()
+    for dz in range(ZS):
+        pick(dz)
+
+    @pl.loop(0, ZS)
+    def _(dz):
+        puts[dz] = onehot(list_row(recv_ref, dz))
+
+    slot_ids = lax.broadcasted_iota(jnp.int32, (BLOCKS, 128), 1).astype(F32)
+    counts = row_to_column(slots_ref[...].astype(F32), BLOCKS)
+    weights[...] = jnp.where(slot_ids < counts, ew_ref[...], 0.0)
 
     wt = wt_ref[...]
     wsend[...] = jnp.zeros_like(wsend)
@@ -259,6 +245,23 @@
         wsend[p, :, :width] = wt[:, p * width:(p + 1) * width]
     wrecv[0] = wsend[hid]
 
+    pl.semaphore_wait(barrier, BLOCKS - 1 + HIDS - 1)
+
+    to_right = remote(mapped, near.at[0], n1_send.at[0], n1_recv.at[0], dom=right)
+    to_left = remote(mapped, near.at[1], n1_send.at[1], n1_recv.at[1], dom=left)
+    to_right.start()
+    to_left.start()
+
+    for p in range(len(PARTS)):
+        @pl.loop(0, ZS - 1)
+        def _(step):
+            ship_four(True, p, offset(step))
+
+        ship_near(True, p)
+
+    for load in loads[6:]:
+        load.wait()
+
     def hid_at(dl, dx):
         return lax.rem(hid // XS + dl, 2) * XS + lax.rem(lax.rem(hid, XS) + dx, XS)
 
@@ -267,10 +270,6 @@
             if dl + dx:
                 peer = hid_at(dl, dx)
                 remote(wsend.at[peer], wrecv.at[XS * dl + (XS - dx) % XS], w_send.at[0], w_recv.at[0], hid=peer).start()
-
-    slot_ids = lax.broadcasted_iota(jnp.int32, (BLOCKS, 128), 1).astype(F32)
-    counts = row_to_column(slots_ref[...].astype(F32), BLOCKS)
-    weights[...] = jnp.where(slot_ids < counts, ew_ref[...], 0.0)
 
     def dense_forward(source, s):
         @pl.loop(0, rows // TILE)
@@ -288,10 +287,6 @@
                 acc[:, cols] += got
 
     dense_forward(mapped, 1)
-
-    @pl.loop(0, ZS)
-    def _(dz):
-        puts[dz] = onehot(list_row(recv_ref, dz))
 
     to_right.wait_recv()
     dense_forward(near.at[0], 0)

time: 57.1 us -> 57 us (level)
  no operation moved by 1% of the time
where the time goes in v8:
time: 57 us; the launch traced here: 56.9 us
  Pallas kernels  56.2 us (99%)
  between operations  0.64 us (1%)
    pallas_call x1, Pallas kernels, on_device(): pl.pallas_call(kernel, out_shape=tuple((pltpu.VMEM(*r) for r in results))...  55.5 us

profile of v8, /device:TPU:1, one launch (start us, length us, event | category | flops | bytes accessed | tf_op | source)
XLA Modules:
  0.0 56.9 jit_solution(6004981767856879306)
XLA Ops:
  0.6 55.5 %shard_map.129 = (bf16[64,1024]{1,0:T(8,128)(2,1)S(1)}, bf16[64,1024]{1,0:T(8,128)(2,1)S(1)}, f32[64,512]{1,0:T(8,128)S(1)}, f32[1,64]{1,0:T(1,128)S(1)}) custom-call(bf16[64,512]{1,0:T(8,128)(2,1)} %bitcast.8, bf16[512,1024]{1,0:T(8,128)(2,1)} %feat_hbm.1, bf16[3072,1024]{1,0:T(8,128)(2,1)} %band_hbm.1, s32[4,12]{1,0:T(4,128)} %bitcast.12, ...), custom_call_target="tpu_custom_call" | custom-call | tf_op jit(solution)/shard_map/pallas_call | solution.py:550
  56.1 0.8 %shard_map.130 = (bf16[64,1024]{1,0:T(8,128)(2,1)}, bf16[64,1024]{1,0:T(8,128)(2,1)}, f32[64,512]{1,0:T(8,128)}, f32[1,64]{1,0:T(1,128)}) custom-call(bf16[64,1024]{1,0:T(8,128)(2,1)S(1)} %get-tuple-element.12.refs_0_, bf16[64,1024]{1,0:T(8,128)(2,1)S(1)} %get-tuple-element.13.refs_1_, f32[64,512]{1,0:T(8,128)S(1)} %get-tuple-element.14.refs_2_, ...), custom_call_target="tpu_custom_call" | custom-call | tf_op jit(solution)/shard_map/pallas_call | solution.py:626
